TPU v7x, 32 devices: a whole 2x2x4 slice. The times are simulated.
32 devices in a mesh: gx: 8 (over z, x), gy: 4 (over y, core).
Axes of the slice: x: 2, y: 2, z: 4, core: 2. Of those that a mesh axis runs over, the one named last changes fastest.
Arguments:
- field: bfloat16 [32, 32, 20, 768], P('gx', 'gy'), may hold values from -6 to 6
- cotangent: bfloat16 [32, 32, 20, 768], P('gx', 'gy'), may hold values from -6 to 6
- spectral_weight: bfloat16 [2, 20, 20, 192, 32, 32], P(None, None, None, 'gx', 'gy'), may hold values from -3 to 3
- point_weight: bfloat16 [20, 20], replicated, may hold values from -1.25 to 1.25
Outputs:
- grad_field: bfloat16 [32, 32, 20, 768], P('gx', 'gy')
- grad_spectral: float32 [2, 20, 20, 192, 32, 32], P(None, None, None, 'gx', 'gy')
All inputs are finite; a program needn't handle non-finite values.
Results may differ from a plain program's by a relative error of at most 0.0057.
Values may be sent and summed in bfloat16 or wider, within the bound.
No kernel may reach another device: no remote copies, remote signals or barrier semaphores. Data moves between devices by JAX's collectives and lax.ppermute only.
A program may use at most 448 MiB of HBM per device.

v0:
```python
from functools import partial
import math

import jax
import jax.numpy as jnp
from jax import lax
from jax.sharding import PartitionSpec as P

C = 20
NZ = 32
NT = 24
KX = 32
KY = 32
KZ = 24
KT = 8


inv_root_two = 1.0 / math.sqrt(2.0)
inv_root_tau = 1.0 / math.sqrt(2.0 * math.pi)


def kept_freq(length, retained):
    series = jnp.arange(retained)
    return jnp.where(series < retained // 2, series, series - retained + length)


def line_angles(length, retained):
    cell_index = jnp.arange(length)
    phases = kept_freq(length, retained)[:, None] * cell_index[None, :] % length
    return phases.astype(jnp.float32) * (2.0 * math.pi / length)


def block_angles():
    cell_total = NZ * NT
    series = jnp.arange(cell_total)
    depth_index = series // NT
    moment = series % NT
    mode_list = jnp.arange(KZ * KT)
    depth_freq = kept_freq(NZ, KZ)[mode_list // KT]
    time_freq = mode_list % KT
    phases = (
        depth_freq[None, :] * depth_index[:, None] % NZ * NT
        + time_freq[None, :] * moment[:, None] % NT * NZ
    )
    return (phases % cell_total).astype(jnp.float32) * (2.0 * math.pi / cell_total)


def mode_scale(mode_list, cell_total):
    return jnp.where(mode_list % KT == 0, 1.0, 2.0).astype(jnp.float32) / cell_total


def twiddle(pattern, cosine, sine, sign, values):
    product = partial(jnp.einsum, pattern, precision=lax.Precision.HIGHEST)
    real_part = values[0]
    imaginary = values[1]
    return jnp.stack(
        [
            product(cosine, real_part) - sign * product(sine, imaginary),
            product(cosine, imaginary) + sign * product(sine, real_part),
        ],
        axis=0,
    )


def channel_mix(spectra, weights):
    widened = weights.astype(jnp.float32)
    product = partial(jnp.einsum, "mkli,iomkl->mklo", precision=lax.Precision.HIGHEST)
    return jnp.stack(
        [
            product(spectra[0], widened[0]) - product(spectra[1], widened[1]),
            product(spectra[0], widened[1]) + product(spectra[1], widened[0]),
        ],
        axis=0,
    )


def weight_grads(forward_spec, hidden_spec):
    product = partial(jnp.einsum, "mkli,mklo->iomkl", precision=lax.Precision.HIGHEST)
    return jnp.stack(
        [
            product(forward_spec[0], hidden_spec[0]) + product(forward_spec[1], hidden_spec[1]),
            product(forward_spec[0], hidden_spec[1]) - product(forward_spec[1], hidden_spec[0]),
        ],
        axis=0,
    )


def back_spectra(hidden_spec, weights):
    widened = weights.astype(jnp.float32)
    product = partial(jnp.einsum, "mklo,iomkl->mkli", precision=lax.Precision.HIGHEST)
    return jnp.stack(
        [
            product(hidden_spec[0], widened[0]) + product(hidden_spec[1], widened[1]),
            product(hidden_spec[1], widened[0]) - product(hidden_spec[0], widened[1]),
        ],
        axis=0,
    )


def gelu_slope(preact):
    return (
        0.5 * (1.0 + jax.scipy.special.erf(preact * inv_root_two))
        + preact * jnp.exp(-0.5 * preact * preact) * inv_root_tau
    )


def per_device(field, cotangent, spectral_weight, point_weight):
    x_local = field.shape[0]
    y_local = field.shape[1]
    groups_x = lax.axis_size("gx")
    groups_y = lax.axis_size("gy")
    rows_x = x_local * groups_x
    rows_y = y_local * groups_y
    mode_total = KZ * KT
    cell_total = rows_x * rows_y * NZ * NT
    angles = block_angles()
    forward_table = jnp.concatenate([jnp.cos(angles), -jnp.sin(angles)], axis=1).astype(
        jnp.bfloat16
    )
    unscaled = jnp.concatenate([jnp.cos(angles).T, -jnp.sin(angles).T], axis=0)
    mode_list = jnp.arange(mode_total)
    factors = mode_scale(mode_list, cell_total)
    scaled = unscaled * jnp.concatenate([factors, factors])[:, None]
    row_angles = line_angles(rows_x, KX)
    column_angles = line_angles(rows_y, KY)
    row_cos = jnp.cos(row_angles)
    row_sin = jnp.sin(row_angles)
    column_cos = jnp.cos(column_angles)
    column_sin = jnp.sin(column_angles)

    def analyze(cells):
        flat_cells = cells.reshape(-1, cells.shape[3])
        return jnp.einsum(
            "rz,zk->kr", flat_cells, forward_table, preferred_element_type=jnp.float32
        )

    def synthesize(spectra, table):
        flattened = spectra.reshape(2 * mode_total, -1)
        cells = jnp.einsum("kr,kz->rz", flattened, table, precision=lax.Precision.HIGHEST)
        return cells.reshape(x_local, y_local, C, -1)

    block = mode_total // groups_x

    def forward(cells):
        spectra = analyze(cells).reshape(2, groups_x, block, x_local, y_local * C)
        spectra = lax.all_to_all(spectra, "gx", split_axis=1, concat_axis=3, tiled=True)
        spectra = spectra.reshape(2, block, rows_x, y_local * C)
        spectra = twiddle("ka,mar->mkr", row_cos, row_sin, -1.0, spectra)
        spectra = spectra.reshape(2, block, KX, y_local, C)
        spectra = lax.all_to_all(spectra, "gy", split_axis=2, concat_axis=3, tiled=True)
        return twiddle("lb,mkbc->mklc", column_cos, column_sin, -1.0, spectra)

    def inverse(spectra, table):
        spectra = twiddle("lb,mklc->mkbc", column_cos, column_sin, 1.0, spectra)
        spectra = lax.all_to_all(spectra, "gy", split_axis=3, concat_axis=2, tiled=True)
        spectra = spectra.reshape(2, block, KX, y_local * C)
        spectra = twiddle("ka,mkr->mar", row_cos, row_sin, 1.0, spectra)
        spectra = lax.all_to_all(spectra, "gx", split_axis=2, concat_axis=1, tiled=True)
        return synthesize(spectra, table)

    forward_spec = forward(field)
    mixed = channel_mix(forward_spec, spectral_weight)
    response = inverse(mixed, scaled)
    preact = response + jnp.einsum(
        "xyiz,io->xyoz", field, point_weight, preferred_element_type=jnp.float32
    )
    hidden = (cotangent.astype(jnp.float32) * gelu_slope(preact)).astype(jnp.bfloat16)
    local_count = forward_spec.shape[1]
    local_modes = lax.axis_index("gx") * local_count + jnp.arange(local_count)
    hidden_spec = forward(hidden) * mode_scale(local_modes, cell_total)[:, None, None, None]
    grad_spectral = weight_grads(forward_spec, hidden_spec)
    backward = inverse(back_spectra(hidden_spec, spectral_weight), unscaled)
    local_part = jnp.einsum(
        "xyoz,io->xyiz", hidden, point_weight, preferred_element_type=jnp.float32
    )
    grad_field = (backward + local_part).astype(jnp.bfloat16)
    return (grad_field, grad_spectral)


def solution(mesh):
    placed = (
        P("gx", "gy", None, None),
        P("gx", "gy", None, None),
        P(None, None, None, "gx", "gy", None),
        P(),
    )
    return jax.shard_map(
        per_device,
        mesh=mesh,
        in_specs=placed,
        out_specs=(P("gx", "gy", None, None), P(None, None, None, "gx", "gy", None)),
        check_vma=False,
    )
```

profile of v0, /device:TPU:0, one launch (start us, length us, event | category | flops | bytes accessed | tf_op | source)
XLA Modules:
  0.0 626.2 jit_solution(16816622037891822352)
XLA Ops:
  4.6 4.4 compare_select_fusion.1
  9.0 10.6 %select_select_fusion = s32[192]{0:T(256)S(1)} fusion(pred[192]{0:T(512)(128)(4,1)S(1)} %compare_reduce_fusion, pred[192]{0:T(512)(128)(4,1)S(1)} %compare_reduce_fusion.1, pred[192]{0:T(512)(128)(4,1)S(1)} %compare_reduce_fusion.2, pred[192]{0:T(512)(128)(4,1)S(1)} %compare_reduce_fusion.3, pred[192]{0:T(512)(128)(4,1)S(1)} %compare_reduce_fusion.4, ...), kind=kLoop, calls=%fused_computation.264 | loop fusion | flops 3264 | bytes 4868 | tf_op jit(solution)/shard_map/gather | solution.py:39
  19.6 3.3 cosine_convert_fusion
  23.8 44.1 %all_to_all.120 = f32[2,8,24,4,160]{4,2,3,0,1:T(8,128)S(1)} all-to-all(f32[2,8,24,4,160]{4,2,3,0,1:T(8,128)S(1)} %fusion.63), channel_id=1, replica_groups=mesh['gx'=8,'gy'=4] {'gx'}, dimensions={1} | all-to-all | bytes 1966080 | tf_op jit(solution)/shard_map/all_to_all | solution.py:146
  76.1 3.0 copy.276
  79.1 3.9 pad_maximum_fusion.1
  83.0 5.8 copy.280
  88.9 5.7 reshape.327
  94.5 16.3 %all_to_all.121 = f32[4,1,61440]{2,1,0:T(1,128)S(1)} all-to-all(f32[4,1,61440]{2,1,0:T(1,128)S(1)} %reshape.327), channel_id=1, replica_groups=mesh['gx'=8,'gy'=4] {'gy'}, dimensions={0} | all-to-all | bytes 1966080 | tf_op jit(solution)/shard_map/all_to_all | solution.py:150
  111.4 3.6 reduce.50
  115.0 6.3 %reshape.328 = f32[32,2,20,8,24]{4,3,2,1,0:T(8,128)} reshape(f32[4,61440]{1,0:T(4,128)S(1)} %reduce.50) | data formatting | bytes 1966080
  121.4 2.9 copy.281
  124.6 4.2 fusion.18
  128.8 4.7 fusion.16
  133.5 4.2 subtract_bitcast_fusion.4
  138.9 4.4 add_bitcast_fusion.4
  144.5 24.1 %fusion = (f32[24,8,32,20]{2,1,0,3:T(8,128)S(1)}, f32[24,8,32,20]{2,1,0,3:T(8,128)S(1)}, f32[24,8,32,20]{2,1,0,3:T(8,128)S(1)}, f32[24,8,32,20]{2,1,0,3:T(8,128)S(1)}) fusion(f32[24,8,32,20]{2,1,0,3:T(8,128)S(1)} %copy.468, bf16[2,20,20,24,8,32]{5,4,3,2,1,0:T(8,128)(2,1)} %param.6, f32[24,8,32,20]{2,1,0,3:T(8,128)S(1)} %copy.469), kind=kLoop, calls=%fused_computation.9 | loop fusion | flops 24084480 | bytes 12779520
  179.9 5.8 copy.296
  185.7 5.7 reshape.329
  191.4 17.1 %all_to_all.122 = f32[4,1,61440]{2,1,0:T(1,128)} all-to-all(f32[4,1,61440]{2,1,0:T(1,128)S(1)} %reshape.329), channel_id=1, replica_groups=mesh['gx'=8,'gy'=4] {'gy'}, dimensions={0} | all-to-all | bytes 1966080 | tf_op jit(solution)/shard_map/all_to_all | solution.py:155
  208.5 4.4 reduce.51
  212.9 6.3 %reshape.330 = f32[32,2,20,8,24]{4,3,2,1,0:T(8,128)} reshape(f32[4,61440]{1,0:T(4,128)S(1)} %reduce.51) | data formatting | bytes 1966080
  219.2 5.5 copy.576
  224.8 2.9 fusion.323
  227.7 5.4 copy.299
  233.1 2.8 squeeze.67
  237.6 5.4 copy.298
  243.0 2.4 squeeze.66
  250.5 3.8 all-to-all-start.3
  254.9 4.8 fusion.102
  259.7 31.6 %all-to-all-done.3 = f32[2,24,32,160]{3,1,0,2:T(8,128)S(1)} async-done(((f32[2,24,32,160]{3,1,0,2:T(8,128)}), f32[2,24,32,160]{3,1,0,2:T(8,128)S(1)}, u32[]{:S(2)}, u32[]{:S(2)}) %all-to-all-start.3) | async-done | bytes 983072 | tf_op jit(solution)/shard_map/all_to_all | solution.py:158
  293.5 3.1 reshape.167
  296.6 2.6 copy.302
  301.5 5.6 fusion.57
  311.2 40.8 %all_to_all.123 = f32[2,8,24,4,160]{4,2,3,0,1:T(8,128)S(1)} all-to-all(f32[2,8,24,4,160]{4,2,3,0,1:T(8,128)S(1)} %fusion.61), channel_id=1, replica_groups=mesh['gx'=8,'gy'=4] {'gx'}, dimensions={1} | all-to-all | bytes 1966080 | tf_op jit(solution)/shard_map/all_to_all | solution.py:146
  356.3 3.0 copy.315
  361.3 3.1 copy.312
  364.4 4.4 pad_maximum_fusion.3
  368.8 5.8 copy.316
  374.6 6.5 %reshape.331 = f32[4,1,61440]{2,1,0:T(1,128)} reshape(f32[32,2,20,8,24]{4,3,2,1,0:T(8,128)} %bitcast.347) | data formatting | bytes 1966080
  381.1 3.9 all-to-all-start.5
  385.0 13.3 %all-to-all-done.5 = f32[4,1,61440]{2,1,0:T(1,128)S(1)} async-done(((f32[4,1,61440]{2,1,0:T(1,128)}), f32[4,1,61440]{2,1,0:T(1,128)S(1)}, u32[]{:S(2)}, u32[]{:S(2)}) %all-to-all-start.5) | async-done | bytes 983072 | tf_op jit(solution)/shard_map/all_to_all | solution.py:150
  398.3 4.5 reduce.52
  402.8 7.5 %reshape.332 = f32[32,2,20,8,24]{4,3,2,1,0:T(8,128)} reshape(f32[4,61440]{1,0:T(4,128)} %reduce.52) | data formatting | bytes 1966080
  410.3 2.9 copy.317
  413.5 4.2 fusion.8
  417.8 4.4 fusion.10
  422.2 4.4 add_bitcast_fusion.2
  426.6 4.5 subtract_bitcast_fusion.2
  434.5 44.9 %add_bitcast_fusion = (f32[1,20,20,24,8,32]{5,4,3,2,1,0:T(8,128)}, f32[1,20,20,24,8,32]{5,4,3,2,1,0:T(8,128)}, f32[24,8,32,20]{2,1,0,3:T(8,128)S(1)}, f32[24,8,3...) fusion(f32[24,8,32,20]{2,1,0,3:T(8,128)S(1)} %copy.471, ...), kind=kLoop, calls=%fused_computation.18 | loop fusion | flops 38830080 | bytes 33423360 | tf_op jit(solution)/shard_map/stack | solution.py:79
  488.4 2.4 pad_maximum_fusion.4
  490.8 5.8 copy.332
  496.6 5.7 reshape.333
  502.3 16.3 %all_to_all.124 = f32[4,1,61440]{2,1,0:T(1,128)S(1)} all-to-all(f32[4,1,61440]{2,1,0:T(1,128)S(1)} %reshape.333), channel_id=1, replica_groups=mesh['gx'=8,'gy'=4] {'gy'}, dimensions={0} | all-to-all | bytes 1966080 | tf_op jit(solution)/shard_map/all_to_all | solution.py:155
  518.5 3.6 reduce.53
  522.1 6.3 %reshape.334 = f32[32,2,20,8,24]{4,3,2,1,0:T(8,128)} reshape(f32[4,61440]{1,0:T(4,128)S(1)} %reduce.53) | data formatting | bytes 1966080
  528.5 5.5 copy.575
  534.0 3.1 fusion.321
  537.1 4.6 copy.335
  543.4 2.9 fusion.132
  546.3 4.4 copy.334
  559.8 3.9 all-to-all-start.7
  563.7 51.5 %pad_maximum_fusion = f32[2,20,20,24,8,32]{5,4,3,2,1,0:T(8,128)} fusion(f32[1,20,20,24,8,32]{5,4,3,2,1,0:T(8,128)} %get-tuple-element.25, f32[1,20,20,24,8,32]{5,4,3,2,1,0:T(8,128)} %get-tuple-element.24), kind=kLoop, calls=%fused_computation | loop fusion | flops 4915200 | bytes 39321600 | tf_op jit(solution)/shard_map/stack | solution.py:79
  620.0 4.1 fusion.55
  (120 shorter events, 79.7 us)
Async XLA Ops:
  0.6 306.5 %copy-start = (bf16[20,20]{1,0:T(8,128)(2,1)S(1)}, bf16[20,20]{1,0:T(8,128)(2,1)}, u32[]{:S(2)}) copy-start(bf16[20,20]{1,0:T(8,128)(2,1)} %param.7) | copy-start | bytes 2404
  0.7 22.4 %copy-start.17 = (s32[192]{0:T(256)}, s32[192]{0:T(256)S(1)}, u32[]{:S(2)}) copy-start(s32[192]{0:T(256)S(1)} %and_select_fusion.2) | copy-start | bytes 2308
  19.6 3.4 copy-start.15
  23.0 44.9 %copy-start.13 = (bf16[768,384]{0,1:T(8,128)(2,1)}, bf16[768,384]{0,1:T(8,128)(2,1)S(1)}, u32[]{:S(2)}) copy-start(bf16[768,384]{0,1:T(8,128)(2,1)S(1)} %pad_maximum_fusion.10) | copy-start | bytes 1769476
  144.5 24.1 %copy-start.1 = (f32[24,8,32,20]{2,1,0,3:T(8,128)}, f32[24,8,32,20]{2,1,0,3:T(8,128)S(1)}, u32[]{:S(2)}) copy-start(f32[24,8,32,20]{2,1,0,3:T(8,128)S(1)} %copy.469) | copy-start | bytes 1474564
  245.3 1.1 copy-start.11
  250.5 40.9 %all-to-all-start.3 = ((f32[2,24,32,160]{3,1,0,2:T(8,128)}), f32[2,24,32,160]{3,1,0,2:T(8,128)S(1)}, u32[]{:S(2)}, u32[]{:S(2)}) async-start(f32[2,24,32,160]{3,1,0,2:T(8,128)} %copy.300), calls=%async_computation.3 | async-start | bytes 3145728 | tf_op jit(solution)/shard_map/all_to_all | solution.py:158
  296.6 4.9 copy-start.5
  296.6 4.9 copy-start.7
  296.6 4.9 copy-start.16
  301.5 5.7 copy-start.12
  301.5 5.7 copy-start.18
  308.9 2.3 copy-start.9
  308.9 1.5 copy-start.14
  381.1 17.2 %all-to-all-start.5 = ((f32[4,1,61440]{2,1,0:T(1,128)}), f32[4,1,61440]{2,1,0:T(1,128)S(1)}, u32[]{:S(2)}, u32[]{:S(2)}) async-start(f32[4,1,61440]{2,1,0:T(1,128)} %reshape.331), calls=%async_computation.5 | async-start | bytes 1966080 | tf_op jit(solution)/shard_map/all_to_all | solution.py:150
  433.0 1.5 copy-start.2
  552.4 2.1 copy-start.4
  552.4 4.2 copy-start.3
  559.8 55.4 %all-to-all-start.7 = ((f32[2,24,32,160]{3,1,0,2:T(8,128)}), f32[2,24,32,160]{3,1,0,2:T(8,128)S(1)}, u32[]{:S(2)}, u32[]{:S(2)}) async-start(f32[2,24,32,160]{3,1,0,2:T(8,128)} %copy.336), calls=%async_computation.7 | async-start | bytes 3145728 | tf_op jit(solution)/shard_map/all_to_all | solution.py:158
  618.2 1.7 copy-start.6
  618.2 1.8 copy-start.8
  620.0 4.1 copy-start.10
where the time goes:
time: 636 us; the launch traced here: 626 us
  other arithmetic  175 us (28%)
  local copies, waits for them, and re-layouts  167 us (26%)
  blocking collectives  135 us (21%)
  matrix products  91.3 us (14%)
  waiting for transfers between devices  44.9 us (7%)
  starting transfers between devices  11.6 us (2%)
    another operation x2, other arithmetic, weight_grads(): jnp.stack([product(forward_spec[0], hidden_spec[0]) + product(forward_spe...  96.3 us
    all_to_all x2, blocking collectives, forward(): lax.all_to_all(spectra, 'gx', split_axis=1, concat_axis=3, tiled=True)  84.8 us
    unnamed x52, local copies, waits for them, and re-layouts  59 us
    all_to_all x2, blocking collectives, inverse(): lax.all_to_all(spectra, 'gy', split_axis=3, concat_axis=2, tiled=True)  33.3 us
    all_to_all x2, waiting for transfers between devices, inverse(): lax.all_to_all(spectra, 'gx', split_axis=2, concat_axis=1, tiled=True)  31.6 us
    another operation x6, local copies, waits for them, and re-layouts, twiddle(): jnp.stack([product(cosine, real_part) - sign * product(sine, imaginary),...  27.4 us
    unnamed x1, other arithmetic  24.1 us
    dot_general x8, matrix products, twiddle(): product(cosine, imaginary) + sign * product(sine, real_part)  22.1 us
  transfers between devices with their start and end apart: 3, of which 2 were waited for; matrix products, arithmetic and copies ran while one was open for 9% of the time, Pallas kernels for 0%

commit v1 on v0

--- a/solution.py
+++ b/solution.py
@@ -3,10 +3,13 @@
 
 import jax
 import jax.numpy as jnp
+import ml_dtypes
+import numpy as np
 from jax import lax
+from jax.experimental import pallas as pl
+from jax.experimental.pallas import tpu as pltpu
 from jax.sharding import PartitionSpec as P
 
-C = 20
 NZ = 32
 NT = 24
 KX = 32
@@ -104,9 +107,10 @@
     )
 
 
-def per_device(field, cotangent, spectral_weight, point_weight):
+def plain_device(field, cotangent, spectral_weight, point_weight):
     x_local = field.shape[0]
     y_local = field.shape[1]
+    channels = field.shape[2]
     groups_x = lax.axis_size("gx")
     groups_y = lax.axis_size("gy")
     rows_x = x_local * groups_x
@@ -137,23 +141,23 @@
     def synthesize(spectra, table):
         flattened = spectra.reshape(2 * mode_total, -1)
         cells = jnp.einsum("kr,kz->rz", flattened, table, precision=lax.Precision.HIGHEST)
-        return cells.reshape(x_local, y_local, C, -1)
+        return cells.reshape(x_local, y_local, channels, -1)
 
     block = mode_total // groups_x
 
     def forward(cells):
-        spectra = analyze(cells).reshape(2, groups_x, block, x_local, y_local * C)
+        spectra = analyze(cells).reshape(2, groups_x, block, x_local, y_local * channels)
         spectra = lax.all_to_all(spectra, "gx", split_axis=1, concat_axis=3, tiled=True)
-        spectra = spectra.reshape(2, block, rows_x, y_local * C)
+        spectra = spectra.reshape(2, block, rows_x, y_local * channels)
         spectra = twiddle("ka,mar->mkr", row_cos, row_sin, -1.0, spectra)
-        spectra = spectra.reshape(2, block, KX, y_local, C)
+        spectra = spectra.reshape(2, block, KX, y_local, channels)
         spectra = lax.all_to_all(spectra, "gy", split_axis=2, concat_axis=3, tiled=True)
         return twiddle("lb,mkbc->mklc", column_cos, column_sin, -1.0, spectra)
 
     def inverse(spectra, table):
         spectra = twiddle("lb,mklc->mkbc", column_cos, column_sin, 1.0, spectra)
         spectra = lax.all_to_all(spectra, "gy", split_axis=3, concat_axis=2, tiled=True)
-        spectra = spectra.reshape(2, block, KX, y_local * C)
+        spectra = spectra.reshape(2, block, KX, y_local * channels)
         spectra = twiddle("ka,mkr->mar", row_cos, row_sin, 1.0, spectra)
         spectra = lax.all_to_all(spectra, "gx", split_axis=2, concat_axis=1, tiled=True)
         return synthesize(spectra, table)
@@ -177,6 +181,510 @@
     return (grad_field, grad_spectral)
 
 
+LANES = 128
+GROUP_ORDER = (0, 2, 1, 3)
+
+
+def kept_freq_np(length, retained):
+    series = np.arange(retained)
+    return np.where(series < retained // 2, series, series - retained + length)
+
+
+def split_table(table):
+    high = table.astype(ml_dtypes.bfloat16)
+    low = (table - high.astype(np.float64)).astype(ml_dtypes.bfloat16)
+    return np.stack([high, low])
+
+
+def cell_table():
+    cells = np.arange(NZ * NT)
+    modes = np.arange(KZ * KT)
+    depth = kept_freq_np(NZ, KZ)[modes // KT][:, None] * (cells // NT)[None, :] % NZ * NT
+    moment = (modes % KT)[:, None] * (cells % NT)[None, :] % NT * NZ
+    angles = 2.0 * np.pi * ((depth + moment) % (NZ * NT)) / (NZ * NT)
+    return split_table(np.concatenate([np.cos(angles), -np.sin(angles)], axis=0))
+
+
+def rotation(length, retained):
+    phases = np.arange(length)[:, None] * kept_freq_np(length, retained)[None, :] % length
+    angles = 2.0 * np.pi * phases / length
+    cosine, sine = np.cos(angles), np.sin(angles)
+    return np.stack([np.stack([cosine, -sine], axis=1), np.stack([sine, cosine], axis=1)], axis=0)
+
+
+def row_table(groups_x, x_local, y_local, groups_y):
+    turn = rotation(groups_x * x_local, KX)
+    turn = turn.reshape(2, groups_x, x_local, 2, groups_y, KX // groups_y)
+    full = np.einsum("psxqgk,yz->spxygqkz", turn, np.eye(y_local))
+    return split_table(full.reshape(groups_x * 2 * x_local * y_local, -1))
+
+
+def column_table(groups_y, y_local, kx_local):
+    turn = rotation(groups_y * y_local, KY).reshape(2, groups_y, y_local, 2, KY)
+    full = np.einsum("psyql,kh->spkyqhl", turn, np.eye(kx_local))
+    return split_table(full.reshape(groups_y * 2 * kx_local * y_local, -1))
+
+
+def scale_table(block, width, cell_total):
+    factors = np.where(np.arange(block) % KT == 0, 1.0, 2.0) / cell_total
+    return np.broadcast_to(factors[:, None], (block, width)).astype(np.float32)
+
+
+def dot(left, right, left_dim=1, right_dim=0):
+    return lax.dot_general(
+        left, right, (((left_dim,), (right_dim,)), ((), ())), preferred_element_type=jnp.float32
+    )
+
+
+def dot_split(left, table, right_dim):
+    return dot(left, table[0], 1, right_dim) + dot(left, table[1], 1, right_dim)
+
+
+def even_lanes(rows, width):
+    lane = lax.broadcasted_iota(jnp.int32, (rows, LANES), 1)
+    return lane // width % 2 == 0
+
+
+def pack_parts(real, imag, width):
+    even = even_lanes(real.shape[0], width)
+    first = jnp.where(even, real, pltpu.roll(imag, width, 1))
+    second = jnp.where(even, pltpu.roll(real, LANES - width, 1), imag)
+    return first, second
+
+
+def unpack_parts(first, second, width):
+    even = even_lanes(first.shape[0], width)
+    real = jnp.where(even, first, pltpu.roll(second, width, 1))
+    imag = jnp.where(even, pltpu.roll(first, LANES - width, 1), second)
+    return real, imag
+
+
+def gather_cells(ref):
+    pieces = [ref[x, g] for g in GROUP_ORDER for x in range(ref.shape[0])]
+    return jnp.concatenate(pieces, axis=0)
+
+
+def store_spectra(spectra, out_ref, width):
+    half = spectra.shape[0] // 2
+    first, second = pack_parts(spectra[:half], spectra[half:], width)
+    groups = out_ref.shape[0]
+    block = half // groups
+    for d in range(groups):
+        out_ref[d, :block] = first[d * block : (d + 1) * block].astype(out_ref.dtype)
+        out_ref[d, block:] = second[d * block : (d + 1) * block].astype(out_ref.dtype)
+
+
+def load_spectra(ref, width):
+    groups = ref.shape[0]
+    block = ref.shape[1] // 2
+    wide = [ref[s].astype(jnp.float32) for s in range(groups)]
+    first = jnp.concatenate([w[:block] for w in wide], axis=0)
+    second = jnp.concatenate([w[block:] for w in wide], axis=0)
+    real, imag = unpack_parts(first, second, width)
+    return jnp.concatenate([real, imag], axis=0).astype(jnp.bfloat16)
+
+
+def analyze_kernel(field_ref, table_ref, out_ref, cells_ref, *, width):
+    cells = gather_cells(field_ref)
+    cells_ref[...] = cells
+    store_spectra(dot(table_ref[0], cells, 1, 1), out_ref, width)
+
+
+def rows_kernel(in_ref, table_ref, out_ref):
+    groups = in_ref.shape[0]
+    half = in_ref.shape[2] // 2
+    lanes = out_ref.shape[2] // 2
+    for c in range(2):
+        left = jnp.concatenate(
+            [in_ref[s, :, c * half : (c + 1) * half] for s in range(groups)], axis=1
+        )
+        result = dot_split(left, table_ref, 0)
+        for g in range(out_ref.shape[0]):
+            out_ref[g, :, c * lanes : (c + 1) * lanes] = result[
+                :, g * lanes : (g + 1) * lanes
+            ].astype(out_ref.dtype)
+
+
+def rows_back_kernel(in_ref, table_ref, out_ref):
+    half = in_ref.shape[2] // 2
+    lanes = out_ref.shape[2] // 2
+    results = []
+    for c in range(2):
+        left = jnp.concatenate(
+            [in_ref[s, :, c * half : (c + 1) * half] for s in range(in_ref.shape[0])], axis=1
+        )
+        results.append(dot_split(left, table_ref, 1))
+    for d in range(out_ref.shape[0]):
+        pair = [result[:, d * lanes : (d + 1) * lanes] for result in results]
+        out_ref[d] = jnp.concatenate(pair, axis=1).astype(out_ref.dtype)
+
+
+def columns_forward(in_ref, table_ref):
+    half = in_ref.shape[2] // 2
+    for c in range(2):
+        left = jnp.concatenate(
+            [in_ref[s, :, c * half : (c + 1) * half] for s in range(in_ref.shape[0])], axis=1
+        )
+        yield c, dot_split(left, table_ref, 0)
+
+
+def columns_back(mixed_ref, table_ref, out_ref):
+    lanes = out_ref.shape[2] // 2
+    for c in range(2):
+        mixed = mixed_ref[c]
+        high = mixed.astype(jnp.bfloat16)
+        low = (mixed - high.astype(jnp.float32)).astype(jnp.bfloat16)
+        result = dot_split(high, table_ref, 1) + dot(low, table_ref[0], 1, 1)
+        for g in range(out_ref.shape[0]):
+            out_ref[g, :, c * lanes : (c + 1) * lanes] = result[
+                :, g * lanes : (g + 1) * lanes
+            ].astype(out_ref.dtype)
+
+
+def mix_kernel(
+    in_ref, table_ref, weight_ref, scale_ref, spec_ref, out_ref, mixed_ref, *, backward
+):
+    step = pl.program_id(0)
+    block, width = scale_ref.shape
+    channels = weight_ref.shape[1] if backward else weight_ref.shape[0]
+    inner = weight_ref.shape[0] if backward else weight_ref.shape[1]
+
+    @pl.when(step == 0)
+    def _():
+        for c, result in columns_forward(in_ref, table_ref):
+            if backward:
+                for r in range(channels // 2):
+                    rows = slice(r * block, (r + 1) * block)
+                    for p in range(2):
+                        lanes = slice(p * width, (p + 1) * width)
+                        spec_ref[c, rows, lanes] = result[rows, lanes] * scale_ref[...]
+            else:
+                spec_ref[c] = result
+
+    for n in range(inner):
+        real = jnp.zeros((block, width), jnp.float32)
+        imag = jnp.zeros((block, width), jnp.float32)
+        for k in range(channels):
+            rows = slice(k // 2 * block, (k // 2 + 1) * block)
+            spec_real = spec_ref[k % 2, rows, :width]
+            spec_imag = spec_ref[k % 2, rows, width:]
+            w = weight_ref.at[n, k] if backward else weight_ref.at[k, n]
+            w_real = w[0].astype(jnp.float32)
+            w_imag = w[1].astype(jnp.float32)
+            if backward:
+                real = real + (spec_real * w_real + spec_imag * w_imag)
+                imag = imag + (spec_imag * w_real - spec_real * w_imag)
+            else:
+                real = real + (spec_real * w_real - spec_imag * w_imag)
+                imag = imag + (spec_real * w_imag + spec_imag * w_real)
+        if not backward:
+            real = real * scale_ref[...]
+            imag = imag * scale_ref[...]
+        rows = pl.ds(pl.multiple_of((step * inner + n) // 2 * block, 8), block)
+        mixed_ref[n % 2, rows, :width] = real
+        mixed_ref[n % 2, rows, width:] = imag
+
+    @pl.when(step == pl.num_programs(0) - 1)
+    def _():
+        columns_back(mixed_ref, table_ref, out_ref)
+
+
+def slope_kernel(
+    in_ref, cells_ref, cot_ref, point_ref, table_ref, out_ref, hidden_ref, *, width
+):
+    spectra = load_spectra(in_ref, width)
+    preact = dot(spectra, table_ref[0], 0, 0) + dot(spectra, table_ref[1], 0, 0)
+    preact = preact + dot(point_ref[...], cells_ref[...])
+    slope = gelu_slope(preact)
+    hidden = (gather_cells(cot_ref).astype(jnp.float32) * slope).astype(jnp.bfloat16)
+    hidden_ref[...] = hidden
+    store_spectra(dot(table_ref[0], hidden, 1, 1), out_ref, width)
+
+
+def final_kernel(in_ref, hidden_ref, point_ref, table_ref, out_ref, *, width):
+    spectra = load_spectra(in_ref, width)
+    total = dot(spectra, table_ref[0], 0, 0) + dot(spectra, table_ref[1], 0, 0)
+    total = total + dot(point_ref[...], hidden_ref[...], 0, 0)
+    x_local, _, y_local, _ = out_ref.shape
+    total = total.astype(out_ref.dtype)
+    for n, g in enumerate(GROUP_ORDER):
+        for x in range(x_local):
+            start = (n * x_local + x) * y_local
+            out_ref[x, g] = total[start : start + y_local]
+
+
+def point_kernel(weight_ref, out_ref, *, width):
+    rows, channels = out_ref.shape[0], weight_ref.shape[0]
+    cell = lax.broadcasted_iota(jnp.int32, (rows, channels), 0) // width
+    slot = cell % 4
+    channel = cell // 4 * 4 + slot // 2 + slot % 2 * 2
+    pick = (channel == lax.broadcasted_iota(jnp.int32, (rows, channels), 1)).astype(jnp.bfloat16)
+    left = dot(pick, weight_ref[...], 1, 1).astype(jnp.bfloat16)
+    full = dot(left, pick, 1, 1)
+    row = lax.broadcasted_iota(jnp.int32, (rows, rows), 0) % width
+    column = lax.broadcasted_iota(jnp.int32, (rows, rows), 1) % width
+    out_ref[...] = jnp.where(row == column, full, 0.0).astype(jnp.bfloat16)
+
+
+def pack_weights_kernel(in_ref, out_ref, wide_ref):
+    _, _, outs, block, kx_local, ky = in_ref.shape
+    rows = outs * block
+    per_tile = LANES // ky
+    wide_ref[:, :ky] = in_ref[0, 0].reshape(rows * kx_local, ky).astype(jnp.float32)
+    lane = lax.broadcasted_iota(jnp.int32, (rows, LANES), 1) // ky
+    for t in range(kx_local // per_tile):
+        packed = None
+        for k in range(per_tile):
+            piece = wide_ref[pl.ds(t * per_tile + k, rows, stride=kx_local), :]
+            if k == 0:
+                packed = piece
+            else:
+                packed = jnp.where(lane == k, pltpu.roll(piece, k * ky, 1), packed)
+        packed = packed.astype(jnp.bfloat16)
+        for o in range(outs):
+            out_ref[0, o, 0, :, t * LANES : (t + 1) * LANES] = packed[o * block : (o + 1) * block]
+
+
+def spread_kernel(in_ref, out_ref):
+    rows = in_ref.shape[1]
+    kx_local, ky = 8, KY
+    for p in range(2):
+        for k in range(kx_local):
+            start = (p * kx_local + k) * ky
+            out_ref[0, p, pl.ds(k, rows, stride=kx_local), :ky] = in_ref[0, :, start : start + ky]
+
+
+def grads_body(f_ref, h_ref, out_ref):
+    channels = out_ref.shape[1]
+
+    def step(i, carry):
+        f_real = f_ref[i % 2, 0, i // 2, 0]
+        f_imag = f_ref[i % 2, 1, i // 2, 0]
+        for o in range(channels):
+            h_real = h_ref[o % 2, 0, o // 2, 0]
+            h_imag = h_ref[o % 2, 1, o // 2, 0]
+            out_ref[0, i, o, 0] = f_real * h_real + f_imag * h_imag
+            out_ref[1, i, o, 0] = f_real * h_imag - f_imag * h_real
+        return carry
+
+    lax.fori_loop(0, channels, step, 0)
+
+
+def grads_first_kernel(f_ref, h_ref, out_ref):
+    grads_body(f_ref, h_ref, out_ref)
+
+
+def grads_rest_kernel(f_ref, h_ref, _, out_ref):
+    grads_body(f_ref, h_ref, out_ref)
+
+
+def whole(shape):
+    return pl.BlockSpec(shape, lambda *_: (0,) * len(shape))
+
+
+def fits(field, weight, groups_x, groups_y):
+    x_local, y_local, channels, cells = field.shape
+    block, kx_local = weight.shape[3:5]
+    return (
+        cells == NZ * NT
+        and x_local * y_local * 4 == LANES
+        and channels % 4 == 0
+        and block % KT == 0
+        and kx_local == 8
+        and y_local == 8
+        and weight.shape[5] * 4 == LANES
+        and block * groups_x == KZ * KT
+    )
+
+
+def fused_device(field, cotangent, weight, point_weight):
+    x_local, y_local, channels, cells = field.shape
+    groups_x = lax.axis_size("gx")
+    groups_y = lax.axis_size("gy")
+    block, kx_local, ky = weight.shape[3:]
+    cell_total = groups_x * x_local * groups_y * y_local * cells
+    width = x_local * y_local
+    tiles = channels // 4
+    rows = channels // 2 * block
+    lanes = 2 * kx_local * y_local
+    plane = kx_local * ky
+    bf16, f32 = jnp.bfloat16, jnp.float32
+    shape = jax.ShapeDtypeStruct
+    params = partial(pltpu.CompilerParams, vmem_limit_bytes=60000 * 1024)
+
+    table = jnp.asarray(cell_table())
+    row_mat = jnp.asarray(row_table(groups_x, x_local, y_local, groups_y))
+    column_mat = jnp.asarray(column_table(groups_y, y_local, kx_local))
+    scale = jnp.asarray(scale_table(block, plane, cell_total))
+
+    cell_block = pl.BlockSpec((x_local, 4, y_local, cells), lambda c: (0, c, 0, 0))
+    flat_block = pl.BlockSpec((LANES, cells), lambda c: (c, 0))
+    spec_block = pl.BlockSpec((groups_x, 2 * block, LANES), lambda c: (0, c, 0))
+    spec_shape = shape((groups_x, rows, LANES), bf16)
+    flat_shape = shape((channels * width, cells), bf16)
+    mid_shape = shape((groups_y, rows, 2 * lanes), bf16)
+
+    field_rows = field.transpose(0, 2, 1, 3)
+    cot_rows = cotangent.transpose(0, 2, 1, 3)
+
+    spectra, flat_field = pl.pallas_call(
+        partial(analyze_kernel, width=width),
+        grid=(tiles,),
+        in_specs=[cell_block, whole(table.shape)],
+        out_specs=[spec_block, flat_block],
+        out_shape=[spec_shape, flat_shape],
+        compiler_params=params(),
+        name="analyze",
+    )(field_rows, table)
+
+    packed = pl.pallas_call(
+        pack_weights_kernel,
+        grid=(channels, 2),
+        in_specs=[
+            pl.BlockSpec((1, 1, channels, block, kx_local, ky), lambda i, p: (p, i, 0, 0, 0, 0))
+        ],
+        out_specs=pl.BlockSpec((1, channels, 1, block, plane), lambda i, p: (i, 0, p, 0, 0)),
+        out_shape=shape((channels, channels, 2, block, plane), bf16),
+        scratch_shapes=[pltpu.VMEM((channels * block * kx_local, LANES), f32)],
+        compiler_params=params(),
+        name="pack_weights",
+    )(weight)
+
+    point = pl.pallas_call(
+        partial(point_kernel, width=width),
+        out_shape=shape((channels * width, channels * width), bf16),
+        compiler_params=params(),
+        name="point",
+    )(point_weight)
+
+    def over_x(values):
+        return lax.all_to_all(values, "gx", 0, 0, tiled=True)
+
+    def over_y(values):
+        return lax.all_to_all(values, "gy", 0, 0, tiled=True)
+
+    def to_rows(values):
+        return pl.pallas_call(
+            rows_kernel,
+            out_shape=mid_shape,
+            compiler_params=params(),
+            name="rows",
+        )(values, row_mat)
+
+    def from_rows(values):
+        return pl.pallas_call(
+            rows_back_kernel,
+            out_shape=spec_shape,
+            compiler_params=params(),
+            name="rows_back",
+        )(values, row_mat)
+
+    def mix(values, backward):
+        if backward:
+            w_block = pl.BlockSpec((2, channels, 2, block, plane), lambda j: (j, 0, 0, 0, 0))
+        else:
+            w_block = pl.BlockSpec((channels, 2, 2, block, plane), lambda j: (0, j, 0, 0, 0))
+        return pl.pallas_call(
+            partial(mix_kernel, backward=backward),
+            grid=(channels // 2,),
+            in_specs=[whole(mid_shape.shape), whole(column_mat.shape), w_block, whole(scale.shape)],
+            out_specs=[whole((2, rows, 2 * plane)), whole(mid_shape.shape)],
+            out_shape=[shape((2, rows, 2 * plane), f32), mid_shape],
+            scratch_shapes=[pltpu.VMEM((2, rows, 2 * plane), f32)],
+            compiler_params=params(),
+            name="mix_back" if backward else "mix",
+        )(values, column_mat, packed, scale)
+
+    def spread(spec):
+        return pl.pallas_call(
+            spread_kernel,
+            grid=(2,),
+            in_specs=[pl.BlockSpec((1, rows, 2 * plane), lambda c: (c, 0, 0))],
+            out_specs=pl.BlockSpec((1, 2, rows * kx_local, ky), lambda c: (c, 0, 0, 0)),
+            out_shape=shape((2, 2, rows * kx_local, ky), f32),
+            compiler_params=params(),
+            name="spread",
+        )(spec).reshape(2, 2, channels // 2, block, kx_local, ky)
+
+    forward_spec, mixed = mix(over_y(to_rows(over_x(spectra))), False)
+    back = over_x(from_rows(over_y(mixed)))
+    hidden_spectra, hidden = pl.pallas_call(
+        partial(slope_kernel, width=width),
+        grid=(tiles,),
+        in_specs=[
+            spec_block,
+            whole(flat_shape.shape),
+            cell_block,
+            pl.BlockSpec((LANES, channels * width), lambda c: (c, 0)),
+            whole(table.shape),
+        ],
+        out_specs=[spec_block, flat_block],
+        out_shape=[spec_shape, flat_shape],
+        compiler_params=params(),
+        name="slope",
+    )(back, flat_field, cot_rows, point, table)
+    hidden_spec, mixed = mix(over_y(to_rows(over_x(hidden_spectra))), True)
+
+    spread_f = spread(forward_spec)
+    spread_h = spread(hidden_spec)
+    tile = (2, 2, channels // 2, 1, kx_local, ky)
+    grad_tile = (2, channels, channels, 1, kx_local, ky)
+    grad_shape = shape((2, channels, channels, block, kx_local, ky), f32)
+    head = block // 3
+
+    def at(offset):
+        return lambda m: (0, 0, 0, m + offset, 0, 0)
+
+    grad_head = pl.pallas_call(
+        grads_first_kernel,
+        grid=(head,),
+        in_specs=[pl.BlockSpec(tile, at(0)), pl.BlockSpec(tile, at(0))],
+        out_specs=pl.BlockSpec(grad_tile, at(0)),
+        out_shape=grad_shape,
+        compiler_params=params(),
+        name="grads_first",
+    )(spread_f, spread_h)
+
+    back = from_rows(over_y(mixed))
+    grad_spectral = pl.pallas_call(
+        grads_rest_kernel,
+        grid=(block - head,),
+        in_specs=[
+            pl.BlockSpec(tile, at(head)),
+            pl.BlockSpec(tile, at(head)),
+            pl.BlockSpec(memory_space=pl.ANY),
+        ],
+        out_specs=pl.BlockSpec(grad_tile, at(head)),
+        out_shape=grad_shape,
+        input_output_aliases={2: 0},
+        compiler_params=params(),
+        name="grads_rest",
+    )(spread_f, spread_h, grad_head)
+    back = over_x(back)
+    grad_field = pl.pallas_call(
+        partial(final_kernel, width=width),
+        grid=(tiles,),
+        in_specs=[
+            spec_block,
+            whole(flat_shape.shape),
+            pl.BlockSpec((channels * width, LANES), lambda c: (0, c)),
+            whole(table.shape),
+        ],
+        out_specs=cell_block,
+        out_shape=shape((x_local, channels, y_local, cells), bf16),
+        compiler_params=params(),
+        name="final",
+    )(back, hidden, point, table)
+    return grad_field.transpose(0, 2, 1, 3), grad_spectral
+
+
+def per_device(field, cotangent, spectral_weight, point_weight):
+    groups = lax.axis_size("gx"), lax.axis_size("gy")
+    if fits(field, spectral_weight, *groups):
+        return fused_device(field, cotangent, spectral_weight, point_weight)
+    return plain_device(field, cotangent, spectral_weight, point_weight)
+
+
 def solution(mesh):
     placed = (
         P("gx", "gy", None, None),

time: 636 us -> 244 us (0.38); the launches traced: 626 us -> 241 us
  other arithmetic: 175 us -> 0 us
  local copies, waits for them, and re-layouts: 167 us -> 2.36 us
  Pallas kernels: 0 us -> 139 us
  matrix products: 91.3 us -> 0 us
  blocking collectives: 135 us -> 76.8 us
  waiting for transfers between devices: 44.9 us -> 11.4 us
    pallas_call x0 -> x15, Pallas kernels: none -> 139 us  [the longest x1 40.2 us: fused_device(): pl.pallas_call(pack_weights_kernel, grid=(channels, 2), in_specs=[pl.Bloc...]
    another operation x9 -> x0, other arithmetic: 113 us -> none  [the longest x2 96.3 us: weight_grads(): jnp.stack([product(forward_spec[0], hidden_spec[0]) + product(forward_spe...]
    dot_general x38 -> x0, matrix products: 91.3 us -> none  [the longest x8 22.1 us: twiddle(): product(cosine, imaginary) + sign * product(sine, real_part)]
    all_to_all x5, blocking collectives: 135 us -> 76.8 us  [the longest x2 38.8 us: over_x(): return lax.all_to_all(values, 'gx', 0, 0, tiled=True)]
    unnamed x52 -> x6, local copies, waits for them, and re-layouts: 59 us -> 2.36 us
    all_to_all x3, waiting for transfers between devices: 44.9 us -> 11.4 us  [the longest x2 11.4 us: over_x(): return lax.all_to_all(values, 'gx', 0, 0, tiled=True)]
    another operation x6 -> x0, local copies, waits for them, and re-layouts: 27.4 us -> none  [twiddle(): jnp.stack([product(cosine, real_part) - sign * product(sine, imaginary),...]
    slice x10 -> x0, local copies, waits for them, and re-layouts: 26.8 us -> none  [the longest x6 16.5 us: twiddle(): real_part = values[0]]
  transfers between devices with their start and end apart: 3 -> 3, of which waited for: 2 -> 1; matrix products, arithmetic and copies ran while one was open for 9% -> 0% of each run, Pallas kernels for 0% -> 34%
where the time goes in v1:
time: 244 us; the launch traced here: 241 us
  Pallas kernels  139 us (57%)
  blocking collectives  76.8 us (31%)
  waiting for transfers between devices  11.4 us (5%)
  starting transfers between devices  10.7 us (4%)
    pallas_call x1, Pallas kernels, fused_device(): pl.pallas_call(pack_weights_kernel, grid=(channels, 2), in_specs=[pl.Bloc...  40.2 us
    all_to_all x2, blocking collectives, over_x(): return lax.all_to_all(values, 'gx', 0, 0, tiled=True)  38.8 us
    all_to_all x3, blocking collectives, over_y(): return lax.all_to_all(values, 'gy', 0, 0, tiled=True)  38 us
    pallas_call x2, Pallas kernels, mix(): pl.pallas_call(partial(mix_kernel, backward=backward), grid=(channels //...  24 us
    pallas_call x1, Pallas kernels, fused_device(): pl.pallas_call(grads_rest_kernel, grid=(block - head,), in_specs=[pl.Bloc...  21.4 us
    pallas_call x1, Pallas kernels, fused_device(): pl.pallas_call(grads_first_kernel, grid=(head,), in_specs=[pl.BlockSpec(t...  11.6 us
    all_to_all x2, waiting for transfers between devices, over_x(): return lax.all_to_all(values, 'gx', 0, 0, tiled=True)  11.4 us
    pallas_call x1, Pallas kernels, fused_device(): pl.pallas_call(partial(slope_kernel, width=width), grid=(tiles,), in_spec...  8.69 us
  transfers between devices with their start and end apart: 3, of which 1 were waited for; matrix products, arithmetic and copies ran while one was open for 0% of the time, Pallas kernels for 34%

profile of v1, /device:TPU:0, one launch (start us, length us, event | category | flops | bytes accessed | tf_op | source)
XLA Modules:
  0.0 240.6 jit_solution(6243617689172079140)
XLA Ops:
  0.6 5.4 %analyze.1 = (bf16[8,240,128]{2,1,0:T(8,128)(2,1)}, bf16[640,768]{1,0:T(8,128)(2,1)}) custom-call(bf16[4,20,8,768]{3,2,1,0:T(8,128)(2,1)} %bitcast.9, bf16[2,384,768]{2,1,0:T(8,128)(2,1)} %constant.8.clone.table_ref), custom_call_target="tpu_custom_call" | custom-call | tf_op jit(solution)/shard_map/analyze/pallas_call | solution.py:530
  6.0 21.2 %all_to_all.40.in_ref = bf16[8,240,128]{2,1,0:T(8,128)(2,1)} all-to-all(bf16[8,240,128]{2,1,0:T(8,128)(2,1)} %get-tuple-element.10), channel_id=1, replica_groups=mesh['gx'=8,'gy'=4] {'gx'}, dimensions={0} | all-to-all | bytes 983040 | tf_op jit(solution)/shard_map/all_to_all | solution.py:561
  27.3 2.9 %rows.2 = bf16[4,240,256]{2,1,0:T(8,128)(2,1)} custom-call(bf16[8,240,128]{2,1,0:T(8,128)(2,1)} %all_to_all.40.in_ref, bf16[2,512,512]{2,1,0:T(8,128)(2,1)} %constant.9.clone.table_ref), custom_call_target="tpu_custom_call" | custom-call | tf_op jit(solution)/shard_map/rows/pallas_call | solution.py:567
  30.1 3.5 %all-to-all-start.1 = ((bf16[4,240,256]{2,1,0:T(8,128)(2,1)}), bf16[4,240,256]{2,1,0:T(8,128)(2,1)S(1)}, u32[]{:S(2)}, u32[]{:S(2)}) async-start(bf16[4,240,256]{2,1,0:T(8,128)(2,1)} %rows.2), calls=%async_computation.1 | async-start | bytes 983040 | tf_op jit(solution)/shard_map/all_to_all | solution.py:564
  33.6 40.2 %pack_weights.1.weight_ref = bf16[20,20,2,24,256]{4,3,2,1,0:T(8,128)(2,1)} custom-call(bf16[2,20,20,24,8,32]{5,4,3,2,1,0:T(8,128)(2,1)} %in_ref.1), custom_call_target="tpu_custom_call" | custom-call | tf_op jit(solution)/shard_map/pack_weights/pallas_call | solution.py:540
  73.8 0.0 all-to-all-done.1.in_ref
  73.8 0.0 copy-start.2
  73.8 0.8 copy-done.2
  74.6 12.1 %mix.1 = (f32[2,240,512]{2,1,0:T(8,128)}, bf16[4,240,256]{2,1,0:T(8,128)(2,1)}) custom-call(bf16[4,240,256]{2,1,0:T(8,128)(2,1)} %copy-done.2, bf16[2,512,512]{2,1,0:T(8,128)(2,1)} %constant.10.clone.table_ref, bf16[20,20,2,24,256]{4,3,2,1,0:T(8,128)(2,1)} %pack_weights.1.weight_ref, f32[24,256]{1,0:T(8,128)} %constant.11.clone.scale_ref), custom_call_target="tpu_custom_call" | custom-call | tf_op jit(solution)/shard_map/mix/pallas_call | solution.py:587
  86.7 12.7 %all_to_all.41.in_ref = bf16[4,240,256]{2,1,0:T(8,128)(2,1)} all-to-all(bf16[4,240,256]{2,1,0:T(8,128)(2,1)} %get-tuple-element.11), channel_id=1, replica_groups=mesh['gx'=8,'gy'=4] {'gy'}, dimensions={0} | all-to-all | bytes 983040 | tf_op jit(solution)/shard_map/all_to_all | solution.py:564
  99.3 3.0 %rows_back.2 = bf16[8,240,128]{2,1,0:T(8,128)(2,1)} custom-call(bf16[4,240,256]{2,1,0:T(8,128)(2,1)} %all_to_all.41.in_ref, bf16[2,512,512]{2,1,0:T(8,128)(2,1)} %constant.9.clone.table_ref), custom_call_target="tpu_custom_call" | custom-call | tf_op jit(solution)/shard_map/rows_back/pallas_call | solution.py:575
  102.3 3.6 %all-to-all-start.3 = ((bf16[8,240,128]{2,1,0:T(8,128)(2,1)}), bf16[8,240,128]{2,1,0:T(8,128)(2,1)S(1)}, u32[]{:S(2)}, u32[]{:S(2)}) async-start(bf16[8,240,128]{2,1,0:T(8,128)(2,1)} %rows_back.2), calls=%async_computation.3 | async-start | bytes 983040 | tf_op jit(solution)/shard_map/all_to_all | solution.py:561
  105.9 2.2 point.1.point_ref
  108.1 11.4 %all-to-all-done.3.in_ref = bf16[8,240,128]{2,1,0:T(8,128)(2,1)S(1)} async-done(((bf16[8,240,128]{2,1,0:T(8,128)(2,1)}), bf16[8,240,128]{2,1,0:T(8,128)(2,1)S(1)}, u32[]{:S(2)}, u32[]{:S(2)}) %all-to-all-start.3) | async-done | bytes 491552 | tf_op jit(solution)/shard_map/all_to_all | solution.py:561
  119.6 0.0 copy-start.1
  119.6 0.8 copy-done.1
  120.4 8.7 %slope.1 = (bf16[8,240,128]{2,1,0:T(8,128)(2,1)}, bf16[640,768]{1,0:T(8,128)(2,1)}) custom-call(bf16[8,240,128]{2,1,0:T(8,128)(2,1)} %copy-done.1, bf16[640,768]{1,0:T(8,128)(2,1)} %get-tuple-element.12.cells_ref, bf16[4,20,8,768]{3,2,1,0:T(8,128)(2,1)} %bitcast.10, bf16[640,640]{1,0:T(8,128)(2,1)} %point.1.point_ref, ...), custom_call_target="tpu_custom_call" | custom-call | tf_op jit(solution)/shard_map/slope/pallas_call | solution.py:611
  129.0 17.6 %all_to_all.42.in_ref = bf16[8,240,128]{2,1,0:T(8,128)(2,1)} all-to-all(bf16[8,240,128]{2,1,0:T(8,128)(2,1)} %get-tuple-element.13), channel_id=1, replica_groups=mesh['gx'=8,'gy'=4] {'gx'}, dimensions={0} | all-to-all | bytes 983040 | tf_op jit(solution)/shard_map/all_to_all | solution.py:561
  146.6 2.9 %rows.3 = bf16[4,240,256]{2,1,0:T(8,128)(2,1)} custom-call(bf16[8,240,128]{2,1,0:T(8,128)(2,1)} %all_to_all.42.in_ref, bf16[2,512,512]{2,1,0:T(8,128)(2,1)} %constant.9.clone.table_ref), custom_call_target="tpu_custom_call" | custom-call | tf_op jit(solution)/shard_map/rows/pallas_call | solution.py:567
  149.5 12.7 %all_to_all.43.in_ref = bf16[4,240,256]{2,1,0:T(8,128)(2,1)} all-to-all(bf16[4,240,256]{2,1,0:T(8,128)(2,1)} %rows.3), channel_id=1, replica_groups=mesh['gx'=8,'gy'=4] {'gy'}, dimensions={0} | all-to-all | bytes 983040 | tf_op jit(solution)/shard_map/all_to_all | solution.py:564
  162.1 12.0 %mix_back.1 = (f32[2,240,512]{2,1,0:T(8,128)}, bf16[4,240,256]{2,1,0:T(8,128)(2,1)}) custom-call(bf16[4,240,256]{2,1,0:T(8,128)(2,1)} %all_to_all.43.in_ref, bf16[2,512,512]{2,1,0:T(8,128)(2,1)} %constant.10.clone.table_ref, bf16[20,20,2,24,256]{4,3,2,1,0:T(8,128)(2,1)} %pack_weights.1.weight_ref, f32[24,256]{1,0:T(8,128)} %constant.11.clone.scale_ref), custom_call_target="tpu_custom_call" | custom-call | tf_op jit(solution)/shard_map/mix_back/pallas_call | solution.py:587
  174.1 12.7 %all_to_all.44.in_ref = bf16[4,240,256]{2,1,0:T(8,128)(2,1)} all-to-all(bf16[4,240,256]{2,1,0:T(8,128)(2,1)} %get-tuple-element.14), channel_id=1, replica_groups=mesh['gx'=8,'gy'=4] {'gy'}, dimensions={0} | all-to-all | bytes 983040 | tf_op jit(solution)/shard_map/all_to_all | solution.py:564
  186.8 3.0 %rows_back.3 = bf16[8,240,128]{2,1,0:T(8,128)(2,1)} custom-call(bf16[4,240,256]{2,1,0:T(8,128)(2,1)} %all_to_all.44.in_ref, bf16[2,512,512]{2,1,0:T(8,128)(2,1)} %constant.9.clone.table_ref), custom_call_target="tpu_custom_call" | custom-call | tf_op jit(solution)/shard_map/rows_back/pallas_call | solution.py:575
  189.8 3.6 %all-to-all-start.7 = ((bf16[8,240,128]{2,1,0:T(8,128)(2,1)}), bf16[8,240,128]{2,1,0:T(8,128)(2,1)S(1)}, u32[]{:S(2)}, u32[]{:S(2)}) async-start(bf16[8,240,128]{2,1,0:T(8,128)(2,1)} %rows_back.3), calls=%async_computation.7 | async-start | bytes 983040 | tf_op jit(solution)/shard_map/all_to_all | solution.py:561
  193.4 3.4 %spread.2 = f32[2,2,1920,32]{3,2,1,0:T(8,128)} custom-call(f32[2,240,512]{2,1,0:T(8,128)} %get-tuple-element.16.in_ref), custom_call_target="tpu_custom_call" | custom-call | tf_op jit(solution)/shard_map/spread/pallas_call | solution.py:599
  196.8 3.5 %spread.3 = f32[2,2,1920,32]{3,2,1,0:T(8,128)} custom-call(f32[2,240,512]{2,1,0:T(8,128)} %get-tuple-element.17.in_ref), custom_call_target="tpu_custom_call" | custom-call | tf_op jit(solution)/shard_map/spread/pallas_call | solution.py:599
  200.3 11.6 %grads_first.1._ = f32[2,20,20,24,8,32]{5,4,3,2,1,0:T(8,128)} custom-call(f32[2,2,10,24,8,32]{5,4,3,2,1,0:T(8,128)} %bitcast.5, f32[2,2,10,24,8,32]{5,4,3,2,1,0:T(8,128)} %bitcast.7), custom_call_target="tpu_custom_call" | custom-call | tf_op jit(solution)/shard_map/grads_first/pallas_call | solution.py:638
  211.9 21.4 %grads_rest.1 = f32[2,20,20,24,8,32]{5,4,3,2,1,0:T(8,128)} custom-call(f32[2,2,10,24,8,32]{5,4,3,2,1,0:T(8,128)} %bitcast.6, f32[2,2,10,24,8,32]{5,4,3,2,1,0:T(8,128)} %bitcast.8, f32[2,20,20,24,8,32]{5,4,3,2,1,0:T(8,128)} %grads_first.1._), custom_call_target="tpu_custom_call", output_to_operand_aliasing={{}: (2, {})} | custom-call | tf_op jit(solution)/shard_map/grads_rest/pallas_call | solution.py:649
  233.4 0.0 all-to-all-done.7.in_ref
  233.4 0.0 copy-start
  233.4 0.8 copy-done
  234.2 6.4 %final.1 = bf16[4,20,8,768]{3,2,1,0:T(8,128)(2,1)} custom-call(bf16[8,240,128]{2,1,0:T(8,128)(2,1)} %copy-done, bf16[640,768]{1,0:T(8,128)(2,1)} %get-tuple-element.15.hidden_ref, bf16[640,640]{1,0:T(8,128)(2,1)} %point.1.point_ref, bf16[2,384,768]{2,1,0:T(8,128)(2,1)} %constant.8.clone.table_ref), custom_call_target="tpu_custom_call" | custom-call | tf_op jit(solution)/shard_map/final/pallas_call | solution.py:664
Async XLA Ops:
  30.1 43.7 %all-to-all-start.1 = ((bf16[4,240,256]{2,1,0:T(8,128)(2,1)}), bf16[4,240,256]{2,1,0:T(8,128)(2,1)S(1)}, u32[]{:S(2)}, u32[]{:S(2)}) async-start(bf16[4,240,256]{2,1,0:T(8,128)(2,1)} %rows.2), calls=%async_computation.1 | async-start | bytes 983040 | tf_op jit(solution)/shard_map/all_to_all | solution.py:564
  73.8 0.8 copy-start.2
  102.3 17.2 %all-to-all-start.3 = ((bf16[8,240,128]{2,1,0:T(8,128)(2,1)}), bf16[8,240,128]{2,1,0:T(8,128)(2,1)S(1)}, u32[]{:S(2)}, u32[]{:S(2)}) async-start(bf16[8,240,128]{2,1,0:T(8,128)(2,1)} %rows_back.2), calls=%async_computation.3 | async-start | bytes 983040 | tf_op jit(solution)/shard_map/all_to_all | solution.py:561
  119.6 0.8 copy-start.1
  189.8 43.6 %all-to-all-start.7 = ((bf16[8,240,128]{2,1,0:T(8,128)(2,1)}), bf16[8,240,128]{2,1,0:T(8,128)(2,1)S(1)}, u32[]{:S(2)}, u32[]{:S(2)}) async-start(bf16[8,240,128]{2,1,0:T(8,128)(2,1)} %rows_back.3), calls=%async_computation.7 | async-start | bytes 983040 | tf_op jit(solution)/shard_map/all_to_all | solution.py:561
  233.4 0.8 copy-start

commit v2 on v1

--- a/solution.py
+++ b/solution.py
@@ -9,6 +9,7 @@
 from jax.experimental import pallas as pl
 from jax.experimental.pallas import tpu as pltpu
 from jax.sharding import PartitionSpec as P
+
 
 NZ = 32
 NT = 24
@@ -345,44 +346,48 @@
     in_ref, table_ref, weight_ref, scale_ref, spec_ref, out_ref, mixed_ref, *, backward
 ):
     step = pl.program_id(0)
-    block, width = scale_ref.shape
+    block = scale_ref.shape[0]
     channels = weight_ref.shape[1] if backward else weight_ref.shape[0]
     inner = weight_ref.shape[0] if backward else weight_ref.shape[1]
+    spans = spec_ref.shape[1] // 2
 
     @pl.when(step == 0)
     def _():
         for c, result in columns_forward(in_ref, table_ref):
-            if backward:
-                for r in range(channels // 2):
-                    rows = slice(r * block, (r + 1) * block)
-                    for p in range(2):
-                        lanes = slice(p * width, (p + 1) * width)
-                        spec_ref[c, rows, lanes] = result[rows, lanes] * scale_ref[...]
-            else:
-                spec_ref[c] = result
-
-    for n in range(inner):
-        real = jnp.zeros((block, width), jnp.float32)
-        imag = jnp.zeros((block, width), jnp.float32)
+            for t in range(2 * spans):
+                piece = result[:, t * LANES : (t + 1) * LANES]
+                if backward:
+                    for r in range(channels // 2):
+                        rows = slice(r * block, (r + 1) * block)
+                        spec_ref[c, t, rows] = piece[rows] * scale_ref[...]
+                else:
+                    spec_ref[c, t] = piece
+
+    for t in range(spans):
+        lanes = slice(t * LANES, (t + 1) * LANES)
+        real = [jnp.zeros((block, LANES), jnp.float32)] * inner
+        imag = [jnp.zeros((block, LANES), jnp.float32)] * inner
         for k in range(channels):
             rows = slice(k // 2 * block, (k // 2 + 1) * block)
-            spec_real = spec_ref[k % 2, rows, :width]
-            spec_imag = spec_ref[k % 2, rows, width:]
-            w = weight_ref.at[n, k] if backward else weight_ref.at[k, n]
-            w_real = w[0].astype(jnp.float32)
-            w_imag = w[1].astype(jnp.float32)
-            if backward:
-                real = real + (spec_real * w_real + spec_imag * w_imag)
-                imag = imag + (spec_imag * w_real - spec_real * w_imag)
-            else:
-                real = real + (spec_real * w_real - spec_imag * w_imag)
-                imag = imag + (spec_real * w_imag + spec_imag * w_real)
-        if not backward:
-            real = real * scale_ref[...]
-            imag = imag * scale_ref[...]
-        rows = pl.ds(pl.multiple_of((step * inner + n) // 2 * block, 8), block)
-        mixed_ref[n % 2, rows, :width] = real
-        mixed_ref[n % 2, rows, width:] = imag
+            spec_real = spec_ref[k % 2, t, rows]
+            spec_imag = spec_ref[k % 2, spans + t, rows]
+            for n in range(inner):
+                w = weight_ref.at[n, k] if backward else weight_ref.at[k, n]
+                w_real = w[0, :, lanes].astype(jnp.float32)
+                w_imag = w[1, :, lanes].astype(jnp.float32)
+                if backward:
+                    real[n] = real[n] + (spec_real * w_real + spec_imag * w_imag)
+                    imag[n] = imag[n] + (spec_imag * w_real - spec_real * w_imag)
+                else:
+                    real[n] = real[n] + (spec_real * w_real - spec_imag * w_imag)
+                    imag[n] = imag[n] + (spec_real * w_imag + spec_imag * w_real)
+        for n in range(inner):
+            if not backward:
+                real[n] = real[n] * scale_ref[...]
+                imag[n] = imag[n] * scale_ref[...]
+            rows = pl.ds(pl.multiple_of((step * inner + n) // 2 * block, 8), block)
+            mixed_ref[n % 2, rows, lanes] = real[n]
+            mixed_ref[n % 2, rows, slice((spans + t) * LANES, (spans + t + 1) * LANES)] = imag[n]
 
     @pl.when(step == pl.num_programs(0) - 1)
     def _():
@@ -426,43 +431,45 @@
     out_ref[...] = jnp.where(row == column, full, 0.0).astype(jnp.bfloat16)
 
 
-def pack_weights_kernel(in_ref, out_ref, wide_ref):
-    _, _, outs, block, kx_local, ky = in_ref.shape
-    rows = outs * block
-    per_tile = LANES // ky
-    wide_ref[:, :ky] = in_ref[0, 0].reshape(rows * kx_local, ky).astype(jnp.float32)
-    lane = lax.broadcasted_iota(jnp.int32, (rows, LANES), 1) // ky
-    for t in range(kx_local // per_tile):
-        packed = None
-        for k in range(per_tile):
-            piece = wide_ref[pl.ds(t * per_tile + k, rows, stride=kx_local), :]
-            if k == 0:
-                packed = piece
-            else:
-                packed = jnp.where(lane == k, pltpu.roll(piece, k * ky, 1), packed)
-        packed = packed.astype(jnp.bfloat16)
-        for o in range(outs):
-            out_ref[0, o, 0, :, t * LANES : (t + 1) * LANES] = packed[o * block : (o + 1) * block]
-
-
-def spread_kernel(in_ref, out_ref):
-    rows = in_ref.shape[1]
-    kx_local, ky = 8, KY
-    for p in range(2):
-        for k in range(kx_local):
-            start = (p * kx_local + k) * ky
-            out_ref[0, p, pl.ds(k, rows, stride=kx_local), :ky] = in_ref[0, :, start : start + ky]
-
-
-def grads_body(f_ref, h_ref, out_ref):
+def pack_body(in_ref, out_ref):
+    for i in range(in_ref.shape[1]):
+        for p in range(2):
+            out_ref[i, :, p] = pltpu.einshape("omky->om(ky)", in_ref[p, i])
+
+
+def pack_first_kernel(in_ref, out_ref):
+    pack_body(in_ref, out_ref)
+
+
+def pack_rest_kernel(in_ref, _, out_ref):
+    pack_body(in_ref, out_ref)
+
+
+def spread_modes(spec_ref, tile_ref, m):
+    count = tile_ref.shape[2] // 8
+    block = spec_ref.shape[2] // count
+    for c in range(2):
+        for p in range(2):
+            for k in range(8):
+                start = (p * 8 + k) * KY
+                piece = spec_ref[c, start // LANES, pl.ds(m, count, stride=block), :]
+                start = start % LANES
+                tile_ref[c, p, pl.ds(k, count, stride=8), :KY] = piece[:, start : start + KY]
+
+
+def grads_body(f_spec_ref, h_spec_ref, out_ref, f_ref, h_ref, first):
     channels = out_ref.shape[1]
+    mode = pl.program_id(0) + first
+    spread_modes(f_spec_ref, f_ref, mode)
+    spread_modes(h_spec_ref, h_ref, mode)
 
     def step(i, carry):
-        f_real = f_ref[i % 2, 0, i // 2, 0]
-        f_imag = f_ref[i % 2, 1, i // 2, 0]
+        rows = pl.ds(pl.multiple_of(i // 2 * 8, 8), 8)
+        f_real = f_ref[i % 2, 0, rows, :KY]
+        f_imag = f_ref[i % 2, 1, rows, :KY]
         for o in range(channels):
-            h_real = h_ref[o % 2, 0, o // 2, 0]
-            h_imag = h_ref[o % 2, 1, o // 2, 0]
+            h_real = h_ref[o % 2, 0, o // 2 * 8 : o // 2 * 8 + 8, :KY]
+            h_imag = h_ref[o % 2, 1, o // 2 * 8 : o // 2 * 8 + 8, :KY]
             out_ref[0, i, o, 0] = f_real * h_real + f_imag * h_imag
             out_ref[1, i, o, 0] = f_real * h_imag - f_imag * h_real
         return carry
@@ -470,12 +477,12 @@
     lax.fori_loop(0, channels, step, 0)
 
 
-def grads_first_kernel(f_ref, h_ref, out_ref):
-    grads_body(f_ref, h_ref, out_ref)
-
-
-def grads_rest_kernel(f_ref, h_ref, _, out_ref):
-    grads_body(f_ref, h_ref, out_ref)
+def grads_first_kernel(f_spec_ref, h_spec_ref, out_ref, f_ref, h_ref):
+    grads_body(f_spec_ref, h_spec_ref, out_ref, f_ref, h_ref, 0)
+
+
+def grads_rest_kernel(f_spec_ref, h_spec_ref, _, out_ref, f_ref, h_ref, *, first):
+    grads_body(f_spec_ref, h_spec_ref, out_ref, f_ref, h_ref, first)
 
 
 def whole(shape):
@@ -510,18 +517,19 @@
     plane = kx_local * ky
     bf16, f32 = jnp.bfloat16, jnp.float32
     shape = jax.ShapeDtypeStruct
-    params = partial(pltpu.CompilerParams, vmem_limit_bytes=60000 * 1024)
+    params = partial(pltpu.CompilerParams, vmem_limit_bytes=58 * 1024 * 1024)
 
     table = jnp.asarray(cell_table())
     row_mat = jnp.asarray(row_table(groups_x, x_local, y_local, groups_y))
     column_mat = jnp.asarray(column_table(groups_y, y_local, kx_local))
-    scale = jnp.asarray(scale_table(block, plane, cell_total))
+    scale = jnp.asarray(scale_table(block, LANES, cell_total))
 
     cell_block = pl.BlockSpec((x_local, 4, y_local, cells), lambda c: (0, c, 0, 0))
     flat_block = pl.BlockSpec((LANES, cells), lambda c: (c, 0))
     spec_block = pl.BlockSpec((groups_x, 2 * block, LANES), lambda c: (0, c, 0))
     spec_shape = shape((groups_x, rows, LANES), bf16)
     flat_shape = shape((channels * width, cells), bf16)
+    full_shape = shape((2, 2 * plane // LANES, rows, LANES), f32)
     mid_shape = shape((groups_y, rows, 2 * lanes), bf16)
 
     field_rows = field.transpose(0, 2, 1, 3)
@@ -537,18 +545,39 @@
         name="analyze",
     )(field_rows, table)
 
+    pack_shape = shape((channels, channels, 2, block, plane), bf16)
+    pack_steps = channels // 2
+    pack_head = pack_steps * 3 // 5
+
+    def pack_specs(offset):
+        return (
+            pl.BlockSpec(
+                (2, 2, channels, block, kx_local, ky), lambda i: (0, i + offset, 0, 0, 0, 0)
+            ),
+            pl.BlockSpec((2, channels, 2, block, plane), lambda i: (i + offset, 0, 0, 0, 0)),
+        )
+
+    source, target = pack_specs(0)
     packed = pl.pallas_call(
-        pack_weights_kernel,
-        grid=(channels, 2),
-        in_specs=[
-            pl.BlockSpec((1, 1, channels, block, kx_local, ky), lambda i, p: (p, i, 0, 0, 0, 0))
-        ],
-        out_specs=pl.BlockSpec((1, channels, 1, block, plane), lambda i, p: (i, 0, p, 0, 0)),
-        out_shape=shape((channels, channels, 2, block, plane), bf16),
-        scratch_shapes=[pltpu.VMEM((channels * block * kx_local, LANES), f32)],
+        pack_first_kernel,
+        grid=(pack_head,),
+        in_specs=[source],
+        out_specs=target,
+        out_shape=pack_shape,
         compiler_params=params(),
-        name="pack_weights",
+        name="pack_first",
     )(weight)
+    source, target = pack_specs(pack_head)
+    packed = pl.pallas_call(
+        pack_rest_kernel,
+        grid=(pack_steps - pack_head,),
+        in_specs=[source, pl.BlockSpec(memory_space=pl.ANY)],
+        out_specs=target,
+        out_shape=pack_shape,
+        input_output_aliases={1: 0},
+        compiler_params=params(),
+        name="pack_rest",
+    )(weight, packed)
 
     point = pl.pallas_call(
         partial(point_kernel, width=width),
@@ -588,23 +617,12 @@
             partial(mix_kernel, backward=backward),
             grid=(channels // 2,),
             in_specs=[whole(mid_shape.shape), whole(column_mat.shape), w_block, whole(scale.shape)],
-            out_specs=[whole((2, rows, 2 * plane)), whole(mid_shape.shape)],
-            out_shape=[shape((2, rows, 2 * plane), f32), mid_shape],
+            out_specs=[whole(full_shape.shape), whole(mid_shape.shape)],
+            out_shape=[full_shape, mid_shape],
             scratch_shapes=[pltpu.VMEM((2, rows, 2 * plane), f32)],
             compiler_params=params(),
             name="mix_back" if backward else "mix",
         )(values, column_mat, packed, scale)
-
-    def spread(spec):
-        return pl.pallas_call(
-            spread_kernel,
-            grid=(2,),
-            in_specs=[pl.BlockSpec((1, rows, 2 * plane), lambda c: (c, 0, 0))],
-            out_specs=pl.BlockSpec((1, 2, rows * kx_local, ky), lambda c: (c, 0, 0, 0)),
-            out_shape=shape((2, 2, rows * kx_local, ky), f32),
-            compiler_params=params(),
-            name="spread",
-        )(spec).reshape(2, 2, channels // 2, block, kx_local, ky)
 
     forward_spec, mixed = mix(over_y(to_rows(over_x(spectra))), False)
     back = over_x(from_rows(over_y(mixed)))
@@ -625,12 +643,11 @@
     )(back, flat_field, cot_rows, point, table)
     hidden_spec, mixed = mix(over_y(to_rows(over_x(hidden_spectra))), True)
 
-    spread_f = spread(forward_spec)
-    spread_h = spread(hidden_spec)
-    tile = (2, 2, channels // 2, 1, kx_local, ky)
     grad_tile = (2, channels, channels, 1, kx_local, ky)
     grad_shape = shape((2, channels, channels, block, kx_local, ky), f32)
-    head = block // 3
+    spec_whole = whole(forward_spec.shape)
+    tiles_scratch = [pltpu.VMEM((2, 2, channels // 2 * kx_local, LANES), f32)] * 2
+    head = block // 4
 
     def at(offset):
         return lambda m: (0, 0, 0, m + offset, 0, 0)
@@ -638,28 +655,26 @@
     grad_head = pl.pallas_call(
         grads_first_kernel,
         grid=(head,),
-        in_specs=[pl.BlockSpec(tile, at(0)), pl.BlockSpec(tile, at(0))],
+        in_specs=[spec_whole, spec_whole],
         out_specs=pl.BlockSpec(grad_tile, at(0)),
         out_shape=grad_shape,
+        scratch_shapes=tiles_scratch,
         compiler_params=params(),
         name="grads_first",
-    )(spread_f, spread_h)
+    )(forward_spec, hidden_spec)
 
     back = from_rows(over_y(mixed))
     grad_spectral = pl.pallas_call(
-        grads_rest_kernel,
+        partial(grads_rest_kernel, first=head),
         grid=(block - head,),
-        in_specs=[
-            pl.BlockSpec(tile, at(head)),
-            pl.BlockSpec(tile, at(head)),
-            pl.BlockSpec(memory_space=pl.ANY),
-        ],
+        in_specs=[spec_whole, spec_whole, pl.BlockSpec(memory_space=pl.ANY)],
         out_specs=pl.BlockSpec(grad_tile, at(head)),
         out_shape=grad_shape,
         input_output_aliases={2: 0},
+        scratch_shapes=tiles_scratch,
         compiler_params=params(),
         name="grads_rest",
-    )(spread_f, spread_h, grad_head)
+    )(forward_spec, hidden_spec, grad_head)
     back = over_x(back)
     grad_field = pl.pallas_call(
         partial(final_kernel, width=width),

time: 244 us -> 221 us (0.906)
  Pallas kernels: 139 us -> 117 us
    pallas_call x5 -> x4, Pallas kernels: 80.2 us -> 59.4 us  [the longest x1 24.4 us: fused_device(): pl.pallas_call(partial(grads_rest_kernel, first=head), grid=(block - head...]
  transfers between devices with their start and end apart: 3 -> 3, of which waited for: 1 -> 1; matrix products, arithmetic and copies ran while one was open for 0% -> 0% of each run, Pallas kernels for 34% -> 28%
where the time goes in v2:
time: 221 us; the launch traced here: 219 us
  Pallas kernels  117 us (53%)
  blocking collectives  76.7 us (35%)
  waiting for transfers between devices  11.5 us (5%)
  starting transfers between devices  10.7 us (5%)
  local copies, waits for them, and re-layouts  2.34 us (1%)
    all_to_all x2, blocking collectives, over_x(): return lax.all_to_all(values, 'gx', 0, 0, tiled=True)  38.7 us
    all_to_all x3, blocking collectives, over_y(): return lax.all_to_all(values, 'gy', 0, 0, tiled=True)  38 us
    pallas_call x1, Pallas kernels, fused_device(): pl.pallas_call(partial(grads_rest_kernel, first=head), grid=(block - head...  24.4 us
    pallas_call x2, Pallas kernels, mix(): pl.pallas_call(partial(mix_kernel, backward=backward), grid=(channels //...  23.6 us
    pallas_call x1, Pallas kernels, fused_device(): pl.pallas_call(pack_first_kernel, grid=(pack_head,), in_specs=[source], o...  14.7 us
    all_to_all x2, waiting for transfers between devices, over_x(): return lax.all_to_all(values, 'gx', 0, 0, tiled=True)  11.5 us
    pallas_call x1, Pallas kernels, fused_device(): pl.pallas_call(pack_rest_kernel, grid=(pack_steps - pack_head,), in_specs...  10.5 us
    pallas_call x1, Pallas kernels, fused_device(): pl.pallas_call(grads_first_kernel, grid=(head,), in_specs=[spec_whole, sp...  9.88 us
  transfers between devices with their start and end apart: 3, of which 1 were waited for; matrix products, arithmetic and copies ran while one was open for 0% of the time, Pallas kernels for 28%

profile of v2, /device:TPU:0, one launch (start us, length us, event | category | flops | bytes accessed | tf_op | source)
XLA Modules:
  0.0 219.2 jit_solution(14532349877523697694)
XLA Ops:
  0.6 5.4 %analyze.1 = (bf16[8,240,128]{2,1,0:T(8,128)(2,1)}, bf16[640,768]{1,0:T(8,128)(2,1)}) custom-call(bf16[4,20,8,768]{3,2,1,0:T(8,128)(2,1)} %bitcast.3, bf16[2,384,768]{2,1,0:T(8,128)(2,1)} %constant.8.clone.table_ref), custom_call_target="tpu_custom_call" | custom-call | tf_op jit(solution)/shard_map/analyze/pallas_call | solution.py:538
  6.0 21.2 %all_to_all.40.in_ref = bf16[8,240,128]{2,1,0:T(8,128)(2,1)} all-to-all(bf16[8,240,128]{2,1,0:T(8,128)(2,1)} %get-tuple-element.10), channel_id=1, replica_groups=mesh['gx'=8,'gy'=4] {'gx'}, dimensions={0} | all-to-all | bytes 983040 | tf_op jit(solution)/shard_map/all_to_all | solution.py:590
  27.3 2.9 %rows.2 = bf16[4,240,256]{2,1,0:T(8,128)(2,1)} custom-call(bf16[8,240,128]{2,1,0:T(8,128)(2,1)} %all_to_all.40.in_ref, bf16[2,512,512]{2,1,0:T(8,128)(2,1)} %constant.9.clone.table_ref), custom_call_target="tpu_custom_call" | custom-call | tf_op jit(solution)/shard_map/rows/pallas_call | solution.py:596
  30.1 3.5 %all-to-all-start.1 = ((bf16[4,240,256]{2,1,0:T(8,128)(2,1)}), bf16[4,240,256]{2,1,0:T(8,128)(2,1)S(1)}, u32[]{:S(2)}, u32[]{:S(2)}) async-start(bf16[4,240,256]{2,1,0:T(8,128)(2,1)} %rows.2), calls=%async_computation.1 | async-start | bytes 983040 | tf_op jit(solution)/shard_map/all_to_all | solution.py:593
  33.6 14.7 %pack_first.1._ = bf16[20,20,2,24,256]{4,3,2,1,0:T(8,128)(2,1)} custom-call(bf16[2,20,20,24,8,32]{5,4,3,2,1,0:T(8,128)(2,1)} %in_ref.3), custom_call_target="tpu_custom_call" | custom-call | tf_op jit(solution)/shard_map/pack_first/pallas_call | solution.py:561
  48.3 10.5 %pack_rest.1.weight_ref = bf16[20,20,2,24,256]{4,3,2,1,0:T(8,128)(2,1)} custom-call(bf16[2,20,20,24,8,32]{5,4,3,2,1,0:T(8,128)(2,1)} %in_ref.3, bf16[20,20,2,24,256]{4,3,2,1,0:T(8,128)(2,1)} %pack_first.1._), custom_call_target="tpu_custom_call", output_to_operand_aliasing={{}: (1, {})} | custom-call | tf_op jit(solution)/shard_map/pack_rest/pallas_call | solution.py:571
  58.7 0.0 all-to-all-done.1.in_ref
  58.7 0.0 copy-start.1
  58.7 0.8 copy-done.1
  59.5 11.8 %mix.1 = (f32[2,4,240,128]{3,2,1,0:T(8,128)}, bf16[4,240,256]{2,1,0:T(8,128)(2,1)}) custom-call(bf16[4,240,256]{2,1,0:T(8,128)(2,1)} %copy-done.1, bf16[2,512,512]{2,1,0:T(8,128)(2,1)} %constant.10.clone.table_ref, bf16[20,20,2,24,256]{4,3,2,1,0:T(8,128)(2,1)} %pack_rest.1.weight_ref, f32[24,128]{1,0:T(8,128)} %constant.11.clone.scale_ref), custom_call_target="tpu_custom_call" | custom-call | tf_op jit(solution)/shard_map/mix/pallas_call | solution.py:616
  71.3 12.7 %all_to_all.41.in_ref = bf16[4,240,256]{2,1,0:T(8,128)(2,1)} all-to-all(bf16[4,240,256]{2,1,0:T(8,128)(2,1)} %get-tuple-element.11), channel_id=1, replica_groups=mesh['gx'=8,'gy'=4] {'gy'}, dimensions={0} | all-to-all | bytes 983040 | tf_op jit(solution)/shard_map/all_to_all | solution.py:593
  84.0 3.0 %rows_back.2 = bf16[8,240,128]{2,1,0:T(8,128)(2,1)} custom-call(bf16[4,240,256]{2,1,0:T(8,128)(2,1)} %all_to_all.41.in_ref, bf16[2,512,512]{2,1,0:T(8,128)(2,1)} %constant.9.clone.table_ref), custom_call_target="tpu_custom_call" | custom-call | tf_op jit(solution)/shard_map/rows_back/pallas_call | solution.py:604
  87.0 3.6 %all-to-all-start.3 = ((bf16[8,240,128]{2,1,0:T(8,128)(2,1)}), bf16[8,240,128]{2,1,0:T(8,128)(2,1)S(1)}, u32[]{:S(2)}, u32[]{:S(2)}) async-start(bf16[8,240,128]{2,1,0:T(8,128)(2,1)} %rows_back.2), calls=%async_computation.3 | async-start | bytes 983040 | tf_op jit(solution)/shard_map/all_to_all | solution.py:590
  90.6 2.2 point.1.point_ref
  92.7 11.5 %all-to-all-done.3.in_ref = bf16[8,240,128]{2,1,0:T(8,128)(2,1)S(1)} async-done(((bf16[8,240,128]{2,1,0:T(8,128)(2,1)}), bf16[8,240,128]{2,1,0:T(8,128)(2,1)S(1)}, u32[]{:S(2)}, u32[]{:S(2)}) %all-to-all-start.3) | async-done | bytes 491552 | tf_op jit(solution)/shard_map/all_to_all | solution.py:590
  104.2 0.0 copy-start.2
  104.2 0.8 copy-done.2
  105.0 8.7 %slope.1 = (bf16[8,240,128]{2,1,0:T(8,128)(2,1)}, bf16[640,768]{1,0:T(8,128)(2,1)}) custom-call(bf16[8,240,128]{2,1,0:T(8,128)(2,1)} %copy-done.2, bf16[640,768]{1,0:T(8,128)(2,1)} %get-tuple-element.12.cells_ref, bf16[4,20,8,768]{3,2,1,0:T(8,128)(2,1)} %bitcast.4, bf16[640,640]{1,0:T(8,128)(2,1)} %point.1.point_ref, ...), custom_call_target="tpu_custom_call" | custom-call | tf_op jit(solution)/shard_map/slope/pallas_call | solution.py:629
  113.7 17.5 %all_to_all.42.in_ref = bf16[8,240,128]{2,1,0:T(8,128)(2,1)} all-to-all(bf16[8,240,128]{2,1,0:T(8,128)(2,1)} %get-tuple-element.13), channel_id=1, replica_groups=mesh['gx'=8,'gy'=4] {'gx'}, dimensions={0} | all-to-all | bytes 983040 | tf_op jit(solution)/shard_map/all_to_all | solution.py:590
  131.2 2.9 %rows.3 = bf16[4,240,256]{2,1,0:T(8,128)(2,1)} custom-call(bf16[8,240,128]{2,1,0:T(8,128)(2,1)} %all_to_all.42.in_ref, bf16[2,512,512]{2,1,0:T(8,128)(2,1)} %constant.9.clone.table_ref), custom_call_target="tpu_custom_call" | custom-call | tf_op jit(solution)/shard_map/rows/pallas_call | solution.py:596
  134.1 12.7 %all_to_all.43.in_ref = bf16[4,240,256]{2,1,0:T(8,128)(2,1)} all-to-all(bf16[4,240,256]{2,1,0:T(8,128)(2,1)} %rows.3), channel_id=1, replica_groups=mesh['gx'=8,'gy'=4] {'gy'}, dimensions={0} | all-to-all | bytes 983040 | tf_op jit(solution)/shard_map/all_to_all | solution.py:593
  146.8 11.7 %mix_back.1 = (f32[2,4,240,128]{3,2,1,0:T(8,128)}, bf16[4,240,256]{2,1,0:T(8,128)(2,1)}) custom-call(bf16[4,240,256]{2,1,0:T(8,128)(2,1)} %all_to_all.43.in_ref, bf16[2,512,512]{2,1,0:T(8,128)(2,1)} %constant.10.clone.table_ref, bf16[20,20,2,24,256]{4,3,2,1,0:T(8,128)(2,1)} %pack_rest.1.weight_ref, f32[24,128]{1,0:T(8,128)} %constant.11.clone.scale_ref), custom_call_target="tpu_custom_call" | custom-call | tf_op jit(solution)/shard_map/mix_back/pallas_call | solution.py:616
  158.5 12.7 %all_to_all.44.in_ref = bf16[4,240,256]{2,1,0:T(8,128)(2,1)} all-to-all(bf16[4,240,256]{2,1,0:T(8,128)(2,1)} %get-tuple-element.14), channel_id=1, replica_groups=mesh['gx'=8,'gy'=4] {'gy'}, dimensions={0} | all-to-all | bytes 983040 | tf_op jit(solution)/shard_map/all_to_all | solution.py:593
  171.2 3.0 %rows_back.3 = bf16[8,240,128]{2,1,0:T(8,128)(2,1)} custom-call(bf16[4,240,256]{2,1,0:T(8,128)(2,1)} %all_to_all.44.in_ref, bf16[2,512,512]{2,1,0:T(8,128)(2,1)} %constant.9.clone.table_ref), custom_call_target="tpu_custom_call" | custom-call | tf_op jit(solution)/shard_map/rows_back/pallas_call | solution.py:604
  174.1 3.6 %all-to-all-start.7 = ((bf16[8,240,128]{2,1,0:T(8,128)(2,1)}), bf16[8,240,128]{2,1,0:T(8,128)(2,1)S(1)}, u32[]{:S(2)}, u32[]{:S(2)}) async-start(bf16[8,240,128]{2,1,0:T(8,128)(2,1)} %rows_back.3), calls=%async_computation.7 | async-start | bytes 983040 | tf_op jit(solution)/shard_map/all_to_all | solution.py:590
  177.8 9.9 %grads_first.1._ = f32[2,20,20,24,8,32]{5,4,3,2,1,0:T(8,128)} custom-call(f32[2,4,240,128]{3,2,1,0:T(8,128)} %get-tuple-element.16.f_spec_ref, f32[2,4,240,128]{3,2,1,0:T(8,128)} %get-tuple-element.17.h_spec_ref), custom_call_target="tpu_custom_call" | custom-call | tf_op jit(solution)/shard_map/grads_first/pallas_call | solution.py:655
  187.7 24.4 %grads_rest.1 = f32[2,20,20,24,8,32]{5,4,3,2,1,0:T(8,128)} custom-call(f32[2,4,240,128]{3,2,1,0:T(8,128)} %get-tuple-element.16.f_spec_ref, f32[2,4,240,128]{3,2,1,0:T(8,128)} %get-tuple-element.17.h_spec_ref, f32[2,20,20,24,8,32]{5,4,3,2,1,0:T(8,128)} %grads_first.1._), custom_call_target="tpu_custom_call", output_to_operand_aliasing={{}: (2, {})} | custom-call | tf_op jit(solution)/shard_map/grads_rest/pallas_call | solution.py:667
  212.1 0.0 all-to-all-done.7.in_ref
  212.1 0.0 copy-start
  212.1 0.8 copy-done
  212.9 6.4 %final.1 = bf16[4,20,8,768]{3,2,1,0:T(8,128)(2,1)} custom-call(bf16[8,240,128]{2,1,0:T(8,128)(2,1)} %copy-done, bf16[640,768]{1,0:T(8,128)(2,1)} %get-tuple-element.15.hidden_ref, bf16[640,640]{1,0:T(8,128)(2,1)} %point.1.point_ref, bf16[2,384,768]{2,1,0:T(8,128)(2,1)} %constant.8.clone.table_ref), custom_call_target="tpu_custom_call" | custom-call | tf_op jit(solution)/shard_map/final/pallas_call | solution.py:679
Async XLA Ops:
  30.1 28.6 %all-to-all-start.1 = ((bf16[4,240,256]{2,1,0:T(8,128)(2,1)}), bf16[4,240,256]{2,1,0:T(8,128)(2,1)S(1)}, u32[]{:S(2)}, u32[]{:S(2)}) async-start(bf16[4,240,256]{2,1,0:T(8,128)(2,1)} %rows.2), calls=%async_computation.1 | async-start | bytes 983040 | tf_op jit(solution)/shard_map/all_to_all | solution.py:593
  58.7 0.8 copy-start.1
  87.0 17.2 %all-to-all-start.3 = ((bf16[8,240,128]{2,1,0:T(8,128)(2,1)}), bf16[8,240,128]{2,1,0:T(8,128)(2,1)S(1)}, u32[]{:S(2)}, u32[]{:S(2)}) async-start(bf16[8,240,128]{2,1,0:T(8,128)(2,1)} %rows_back.2), calls=%async_computation.3 | async-start | bytes 983040 | tf_op jit(solution)/shard_map/all_to_all | solution.py:590
  104.2 0.8 copy-start.2
  174.1 37.9 %all-to-all-start.7 = ((bf16[8,240,128]{2,1,0:T(8,128)(2,1)}), bf16[8,240,128]{2,1,0:T(8,128)(2,1)S(1)}, u32[]{:S(2)}, u32[]{:S(2)}) async-start(bf16[8,240,128]{2,1,0:T(8,128)(2,1)} %rows_back.3), calls=%async_computation.7 | async-start | bytes 983040 | tf_op jit(solution)/shard_map/all_to_all | solution.py:590
  212.1 0.8 copy-start

commit v3 on v2

--- a/solution.py
+++ b/solution.py
@@ -191,6 +191,13 @@
     return np.where(series < retained // 2, series, series - retained + length)
 
 
+TURN_SCALE = 1.62445
+
+
+def scaled_table(table):
+    return (table * TURN_SCALE).astype(ml_dtypes.bfloat16)
+
+
 def split_table(table):
     high = table.astype(ml_dtypes.bfloat16)
     low = (table - high.astype(np.float64)).astype(ml_dtypes.bfloat16)
@@ -217,13 +224,13 @@
     turn = rotation(groups_x * x_local, KX)
     turn = turn.reshape(2, groups_x, x_local, 2, groups_y, KX // groups_y)
     full = np.einsum("psxqgk,yz->spxygqkz", turn, np.eye(y_local))
-    return split_table(full.reshape(groups_x * 2 * x_local * y_local, -1))
+    return scaled_table(full.reshape(groups_x * 2 * x_local * y_local, -1))
 
 
 def column_table(groups_y, y_local, kx_local):
     turn = rotation(groups_y * y_local, KY).reshape(2, groups_y, y_local, 2, KY)
     full = np.einsum("psyql,kh->spkyqhl", turn, np.eye(kx_local))
-    return split_table(full.reshape(groups_y * 2 * kx_local * y_local, -1))
+    return scaled_table(full.reshape(groups_y * 2 * kx_local * y_local, -1))
 
 
 def scale_table(block, width, cell_total):
@@ -237,8 +244,27 @@
     )
 
 
-def dot_split(left, table, right_dim):
-    return dot(left, table[0], 1, right_dim) + dot(left, table[1], 1, right_dim)
+def turn(left, table_ref, right_dim):
+    if left.dtype == jnp.bfloat16:
+        return dot(left, table_ref[...], 1, right_dim) * (1.0 / TURN_SCALE)
+    high = left.astype(jnp.bfloat16)
+    low = (left - high.astype(jnp.float32)).astype(jnp.bfloat16)
+    both = dot(jnp.concatenate([high, low], axis=0), table_ref[...], 1, right_dim)
+    count = left.shape[0]
+    return (both[:count] + both[count:]) * (1.0 / TURN_SCALE)
+
+
+def joined(in_ref):
+    half = in_ref.shape[2] // 2
+    return jnp.concatenate(
+        [
+            jnp.concatenate(
+                [in_ref[s, :, c * half : (c + 1) * half] for s in range(in_ref.shape[0])], axis=1
+            )
+            for c in range(2)
+        ],
+        axis=0,
+    )
 
 
 def even_lanes(rows, width):
@@ -285,65 +311,82 @@
     return jnp.concatenate([real, imag], axis=0).astype(jnp.bfloat16)
 
 
+def store_tiles(spectra, out_ref, width):
+    rows = out_ref.shape[1] // (spectra.shape[1] // LANES)
+    for c in range(spectra.shape[1] // LANES):
+        store_spectra(
+            spectra[:, c * LANES : (c + 1) * LANES],
+            out_ref.at[:, c * rows : (c + 1) * rows],
+            width,
+        )
+
+
+def load_tiles(in_ref, tiles, width):
+    rows = in_ref.shape[1] // tiles
+    pieces = [load_spectra(in_ref.at[:, c * rows : (c + 1) * rows], width) for c in range(tiles)]
+    return jnp.concatenate(pieces, axis=1)
+
+
 def analyze_kernel(field_ref, table_ref, out_ref, cells_ref, *, width):
-    cells = gather_cells(field_ref)
-    cells_ref[...] = cells
-    store_spectra(dot(table_ref[0], cells, 1, 1), out_ref, width)
+    for c in range(field_ref.shape[1] // 4):
+        cells_ref[c * LANES : (c + 1) * LANES] = gather_cells(field_ref.at[:, 4 * c : 4 * c + 4])
+    store_tiles(dot(table_ref[0], cells_ref[...], 1, 1), out_ref, width)
 
 
 def rows_kernel(in_ref, table_ref, out_ref):
-    groups = in_ref.shape[0]
-    half = in_ref.shape[2] // 2
     lanes = out_ref.shape[2] // 2
+    rows = in_ref.shape[1]
+    result = turn(joined(in_ref), table_ref, 0).astype(out_ref.dtype)
     for c in range(2):
-        left = jnp.concatenate(
-            [in_ref[s, :, c * half : (c + 1) * half] for s in range(groups)], axis=1
-        )
-        result = dot_split(left, table_ref, 0)
         for g in range(out_ref.shape[0]):
             out_ref[g, :, c * lanes : (c + 1) * lanes] = result[
-                :, g * lanes : (g + 1) * lanes
-            ].astype(out_ref.dtype)
+                c * rows : (c + 1) * rows, g * lanes : (g + 1) * lanes
+            ]
 
 
 def rows_back_kernel(in_ref, table_ref, out_ref):
-    half = in_ref.shape[2] // 2
     lanes = out_ref.shape[2] // 2
-    results = []
+    rows = in_ref.shape[1]
+    result = turn(joined(in_ref), table_ref, 1)
+    for d in range(out_ref.shape[0]):
+        pair = [
+            result[c * rows : (c + 1) * rows, d * lanes : (d + 1) * lanes] for c in range(2)
+        ]
+        out_ref[d] = jnp.concatenate(pair, axis=1).astype(out_ref.dtype)
+
+
+def columns_forward(in_ref, table_ref):
+    rows = in_ref.shape[1]
+    result = turn(joined(in_ref), table_ref, 0)
     for c in range(2):
-        left = jnp.concatenate(
-            [in_ref[s, :, c * half : (c + 1) * half] for s in range(in_ref.shape[0])], axis=1
-        )
-        results.append(dot_split(left, table_ref, 1))
-    for d in range(out_ref.shape[0]):
-        pair = [result[:, d * lanes : (d + 1) * lanes] for result in results]
-        out_ref[d] = jnp.concatenate(pair, axis=1).astype(out_ref.dtype)
-
-
-def columns_forward(in_ref, table_ref):
-    half = in_ref.shape[2] // 2
-    for c in range(2):
-        left = jnp.concatenate(
-            [in_ref[s, :, c * half : (c + 1) * half] for s in range(in_ref.shape[0])], axis=1
-        )
-        yield c, dot_split(left, table_ref, 0)
+        yield c, result[c * rows : (c + 1) * rows]
 
 
 def columns_back(mixed_ref, table_ref, out_ref):
     lanes = out_ref.shape[2] // 2
+    rows = mixed_ref.shape[1]
+    mixed = jnp.concatenate([mixed_ref[0], mixed_ref[1]], axis=0)
+    result = turn(mixed, table_ref, 1).astype(out_ref.dtype)
     for c in range(2):
-        mixed = mixed_ref[c]
-        high = mixed.astype(jnp.bfloat16)
-        low = (mixed - high.astype(jnp.float32)).astype(jnp.bfloat16)
-        result = dot_split(high, table_ref, 1) + dot(low, table_ref[0], 1, 1)
         for g in range(out_ref.shape[0]):
             out_ref[g, :, c * lanes : (c + 1) * lanes] = result[
-                :, g * lanes : (g + 1) * lanes
-            ].astype(out_ref.dtype)
+                c * rows : (c + 1) * rows, g * lanes : (g + 1) * lanes
+            ]
+
+
+def mix_back_kernel(
+    in_ref, table_ref, weight_ref, scale_ref, other_ref, out_ref, spec_ref, grad_ref,
+    mixed_ref, f_ref, h_ref,
+):
+    mix_kernel(
+        in_ref, table_ref, weight_ref, scale_ref, out_ref, spec_ref, mixed_ref, backward=True,
+        extra=lambda: grads_body(other_ref, spec_ref, grad_ref, f_ref, h_ref, 0),
+    )
 
 
 def mix_kernel(
-    in_ref, table_ref, weight_ref, scale_ref, spec_ref, out_ref, mixed_ref, *, backward
+    in_ref, table_ref, weight_ref, scale_ref, out_ref, spec_ref, mixed_ref, *, backward,
+    extra=None,
 ):
     step = pl.program_id(0)
     block = scale_ref.shape[0]
@@ -362,6 +405,9 @@
                         spec_ref[c, t, rows] = piece[rows] * scale_ref[...]
                 else:
                     spec_ref[c, t] = piece
+
+    if extra is not None:
+        extra()
 
     for t in range(spans):
         lanes = slice(t * LANES, (t + 1) * LANES)
@@ -394,28 +440,42 @@
         columns_back(mixed_ref, table_ref, out_ref)
 
 
+def synthesize(in_ref, table_ref, tiles, width):
+    spectra = load_tiles(in_ref, tiles, width)
+    return dot(spectra, table_ref[0], 0, 0) + dot(spectra, table_ref[1], 0, 0)
+
+
 def slope_kernel(
-    in_ref, cells_ref, cot_ref, point_ref, table_ref, out_ref, hidden_ref, *, width
+    in_ref, cells_ref, cot_ref, point_ref, table_ref, out_ref, hidden_ref, preact_ref, *, width
 ):
-    spectra = load_spectra(in_ref, width)
-    preact = dot(spectra, table_ref[0], 0, 0) + dot(spectra, table_ref[1], 0, 0)
-    preact = preact + dot(point_ref[...], cells_ref[...])
-    slope = gelu_slope(preact)
-    hidden = (gather_cells(cot_ref).astype(jnp.float32) * slope).astype(jnp.bfloat16)
-    hidden_ref[...] = hidden
-    store_spectra(dot(table_ref[0], hidden, 1, 1), out_ref, width)
+    tiles = cells_ref.shape[0] // LANES
+    preact_ref[...] = synthesize(in_ref, table_ref, tiles, width) + dot(
+        point_ref[...], cells_ref[...]
+    )
+
+    def step(c, carry):
+        rows = pl.ds(pl.multiple_of(c * LANES, LANES), LANES)
+        slope = gelu_slope(preact_ref[rows])
+        pieces = [cot_ref[x, 4 * c + g] for g in GROUP_ORDER for x in range(cot_ref.shape[0])]
+        cot = jnp.concatenate(pieces, axis=0).astype(jnp.float32)
+        hidden_ref[rows] = (cot * slope).astype(jnp.bfloat16)
+        return carry
+
+    lax.fori_loop(0, tiles, step, 0)
+    store_tiles(dot(table_ref[0], hidden_ref[...], 1, 1), out_ref, width)
 
 
 def final_kernel(in_ref, hidden_ref, point_ref, table_ref, out_ref, *, width):
-    spectra = load_spectra(in_ref, width)
-    total = dot(spectra, table_ref[0], 0, 0) + dot(spectra, table_ref[1], 0, 0)
+    tiles = hidden_ref.shape[0] // LANES
+    total = synthesize(in_ref, table_ref, tiles, width)
     total = total + dot(point_ref[...], hidden_ref[...], 0, 0)
-    x_local, _, y_local, _ = out_ref.shape
+    x_local, channels, y_local, _ = out_ref.shape
     total = total.astype(out_ref.dtype)
-    for n, g in enumerate(GROUP_ORDER):
+    for n in range(channels):
+        channel = n // 4 * 4 + GROUP_ORDER[n % 4]
         for x in range(x_local):
             start = (n * x_local + x) * y_local
-            out_ref[x, g] = total[start : start + y_local]
+            out_ref[x, channel] = total[start : start + y_local]
 
 
 def point_kernel(weight_ref, out_ref, *, width):
@@ -477,12 +537,40 @@
     lax.fori_loop(0, channels, step, 0)
 
 
-def grads_first_kernel(f_spec_ref, h_spec_ref, out_ref, f_ref, h_ref):
-    grads_body(f_spec_ref, h_spec_ref, out_ref, f_ref, h_ref, 0)
-
-
 def grads_rest_kernel(f_spec_ref, h_spec_ref, _, out_ref, f_ref, h_ref, *, first):
     grads_body(f_spec_ref, h_spec_ref, out_ref, f_ref, h_ref, first)
+
+
+def routed_kernel(me_ref, *refs, kernel, receive, send, counts, gated):
+    refs = list(refs)
+    taken = receive[1] if receive else 1
+    sources, refs = refs[:taken], refs[taken:]
+    more_in, refs = refs[: counts[0]], refs[counts[0] :]
+    taken = send[1] if send else 1
+    targets, refs = refs[:taken], refs[taken:]
+    more_out, refs = refs[: counts[1]], refs[counts[1] :]
+    in_ref, out_ref = sources[0], targets[0]
+    if send:
+        out_ref = refs.pop()
+    if receive:
+        in_ref = refs.pop()
+
+    def collect():
+        for k, source in enumerate(sources):
+            axis, groups = receive
+            in_ref[lax.rem(me_ref[axis] + (groups - k), groups)] = source[...]
+
+    def spread():
+        for k, target in enumerate(targets):
+            axis, groups = send
+            target[...] = out_ref[lax.rem(me_ref[axis] + k, groups)]
+
+    if receive:
+        pl.when(pl.program_id(0) == 0)(collect) if gated else collect()
+    kernel(in_ref, *more_in, out_ref, *more_out, *refs)
+    if send:
+        last = pl.num_programs(0) - 1
+        pl.when(pl.program_id(0) == last)(spread) if gated else spread()
 
 
 def whole(shape):
@@ -497,6 +585,7 @@
         and x_local * y_local * 4 == LANES
         and channels % 4 == 0
         and block % KT == 0
+        and block > channels
         and kx_local == 8
         and y_local == 8
         and weight.shape[5] * 4 == LANES
@@ -511,7 +600,6 @@
     block, kx_local, ky = weight.shape[3:]
     cell_total = groups_x * x_local * groups_y * y_local * cells
     width = x_local * y_local
-    tiles = channels // 4
     rows = channels // 2 * block
     lanes = 2 * kx_local * y_local
     plane = kx_local * ky
@@ -524,22 +612,66 @@
     column_mat = jnp.asarray(column_table(groups_y, y_local, kx_local))
     scale = jnp.asarray(scale_table(block, LANES, cell_total))
 
-    cell_block = pl.BlockSpec((x_local, 4, y_local, cells), lambda c: (0, c, 0, 0))
-    flat_block = pl.BlockSpec((LANES, cells), lambda c: (c, 0))
-    spec_block = pl.BlockSpec((groups_x, 2 * block, LANES), lambda c: (0, c, 0))
     spec_shape = shape((groups_x, rows, LANES), bf16)
     flat_shape = shape((channels * width, cells), bf16)
     full_shape = shape((2, 2 * plane // LANES, rows, LANES), f32)
     mid_shape = shape((groups_y, rows, 2 * lanes), bf16)
 
+    me = jnp.stack([lax.axis_index("gx"), lax.axis_index("gy")]).astype(jnp.int32)
+    axes = {"gx": (0, groups_x), "gy": (1, groups_y)}
+
+    def route(
+        kernel, values, more, in_block, out_block, out_shape, more_specs, more_outs,
+        receive=None, send=None, grid=(1,), scratch=(), gated=False,
+    ):
+        def single(spec):
+            index = spec.index_map
+            return pl.BlockSpec(spec.block_shape[1:], lambda *at: index(*at)[1:])
+
+        scratch = list(scratch)
+        in_specs, out_specs, out_shapes = [in_block], [out_block], [out_shape]
+        if receive:
+            in_specs = [single(in_block)] * axes[receive][1]
+            scratch.append(pltpu.VMEM(in_block.block_shape, bf16))
+        if send:
+            groups = axes[send][1]
+            out_specs = [single(out_block)] * groups
+            out_shapes = [shape(out_shape.shape[1:], out_shape.dtype)] * groups
+            scratch.append(pltpu.VMEM(out_block.block_shape, bf16))
+        body = partial(
+            routed_kernel,
+            kernel=kernel,
+            receive=receive and axes[receive],
+            send=send and axes[send],
+            counts=(len(more), len(more_outs)),
+            gated=gated,
+        )
+        results = pl.pallas_call(
+            body,
+            grid=grid,
+            in_specs=[pl.BlockSpec(memory_space=pltpu.SMEM)] + in_specs + list(more_specs),
+            out_specs=out_specs + [spec for spec, _ in more_outs],
+            out_shape=out_shapes + [item for _, item in more_outs],
+            scratch_shapes=scratch,
+            compiler_params=params(),
+        )(me, *(values if receive else [values]), *more)
+        if send:
+            return [list(results[:groups])] + list(results[groups:])
+        return list(results)
+
+    def ring(blocks, axis):
+        groups = axes[axis][1]
+        received = list(blocks)
+        for k in sorted(range(1, groups), key=lambda k: -min(k, groups - k)):
+            pairs = [(s, (s + k) % groups) for s in range(groups)]
+            received[k] = lax.ppermute(blocks[k], axis, pairs)
+        return received
+
     field_rows = field.transpose(0, 2, 1, 3)
     cot_rows = cotangent.transpose(0, 2, 1, 3)
 
     spectra, flat_field = pl.pallas_call(
         partial(analyze_kernel, width=width),
-        grid=(tiles,),
-        in_specs=[cell_block, whole(table.shape)],
-        out_specs=[spec_block, flat_block],
         out_shape=[spec_shape, flat_shape],
         compiler_params=params(),
         name="analyze",
@@ -592,100 +724,83 @@
     def over_y(values):
         return lax.all_to_all(values, "gy", 0, 0, tiled=True)
 
-    def to_rows(values):
-        return pl.pallas_call(
-            rows_kernel,
-            out_shape=mid_shape,
-            compiler_params=params(),
-            name="rows",
-        )(values, row_mat)
-
-    def from_rows(values):
-        return pl.pallas_call(
-            rows_back_kernel,
-            out_shape=spec_shape,
-            compiler_params=params(),
-            name="rows_back",
-        )(values, row_mat)
-
-    def mix(values, backward):
-        if backward:
-            w_block = pl.BlockSpec((2, channels, 2, block, plane), lambda j: (j, 0, 0, 0, 0))
-        else:
-            w_block = pl.BlockSpec((channels, 2, 2, block, plane), lambda j: (0, j, 0, 0, 0))
-        return pl.pallas_call(
-            partial(mix_kernel, backward=backward),
-            grid=(channels // 2,),
-            in_specs=[whole(mid_shape.shape), whole(column_mat.shape), w_block, whole(scale.shape)],
-            out_specs=[whole(full_shape.shape), whole(mid_shape.shape)],
-            out_shape=[full_shape, mid_shape],
-            scratch_shapes=[pltpu.VMEM((2, rows, 2 * plane), f32)],
-            compiler_params=params(),
-            name="mix_back" if backward else "mix",
-        )(values, column_mat, packed, scale)
-
-    forward_spec, mixed = mix(over_y(to_rows(over_x(spectra))), False)
-    back = over_x(from_rows(over_y(mixed)))
-    hidden_spectra, hidden = pl.pallas_call(
-        partial(slope_kernel, width=width),
-        grid=(tiles,),
-        in_specs=[
-            spec_block,
-            whole(flat_shape.shape),
-            cell_block,
-            pl.BlockSpec((LANES, channels * width), lambda c: (c, 0)),
-            whole(table.shape),
-        ],
-        out_specs=[spec_block, flat_block],
-        out_shape=[spec_shape, flat_shape],
-        compiler_params=params(),
-        name="slope",
-    )(back, flat_field, cot_rows, point, table)
-    hidden_spec, mixed = mix(over_y(to_rows(over_x(hidden_spectra))), True)
+    spec_full, mid_full = whole(spec_shape.shape), whole(mid_shape.shape)
+
+    def to_rows(values, receive, send):
+        kept = shape(mid_shape.shape, bf16 if send else f32)
+        return route(
+            rows_kernel, values, [row_mat], spec_full, mid_full, kept,
+            [whole(row_mat.shape)], [], receive, send,
+        )[0]
+
+    def from_rows(values, receive, send):
+        return route(
+            rows_back_kernel, values, [row_mat], mid_full, spec_full, spec_shape,
+            [whole(row_mat.shape)], [], receive, send,
+        )[0]
 
     grad_tile = (2, channels, channels, 1, kx_local, ky)
     grad_shape = shape((2, channels, channels, block, kx_local, ky), f32)
-    spec_whole = whole(forward_spec.shape)
     tiles_scratch = [pltpu.VMEM((2, 2, channels // 2 * kx_local, LANES), f32)] * 2
-    head = block // 4
+    mix_scratch = pltpu.VMEM((2, rows, 2 * plane), f32)
+    spec_whole = whole(full_shape.shape)
 
     def at(offset):
         return lambda m: (0, 0, 0, m + offset, 0, 0)
 
-    grad_head = pl.pallas_call(
-        grads_first_kernel,
-        grid=(head,),
-        in_specs=[spec_whole, spec_whole],
-        out_specs=pl.BlockSpec(grad_tile, at(0)),
-        out_shape=grad_shape,
-        scratch_shapes=tiles_scratch,
-        compiler_params=params(),
-        name="grads_first",
-    )(forward_spec, hidden_spec)
-
-    back = from_rows(over_y(mixed))
-    grad_spectral = pl.pallas_call(
-        partial(grads_rest_kernel, first=head),
-        grid=(block - head,),
-        in_specs=[spec_whole, spec_whole, pl.BlockSpec(memory_space=pl.ANY)],
-        out_specs=pl.BlockSpec(grad_tile, at(head)),
-        out_shape=grad_shape,
-        input_output_aliases={2: 0},
-        scratch_shapes=tiles_scratch,
-        compiler_params=params(),
-        name="grads_rest",
-    )(forward_spec, hidden_spec, grad_head)
+    def mix(values, send):
+        w_block = pl.BlockSpec((channels, 2, 2, block, plane), lambda j: (0, j, 0, 0, 0))
+        return route(
+            partial(mix_kernel, backward=False), values, [column_mat, packed, scale],
+            mid_full, mid_full, mid_shape,
+            [whole(column_mat.shape), w_block, whole(scale.shape)],
+            [(spec_whole, full_shape)], None, send, grid=(channels // 2,),
+            scratch=[mix_scratch], gated=True,
+        )
+
+    def mix_back(values, spec, receive):
+        w_block = pl.BlockSpec((2, channels, 2, block, plane), lambda j: (j, 0, 0, 0, 0))
+        return route(
+            mix_back_kernel, values, [column_mat, packed, scale, spec],
+            mid_full, mid_full, mid_shape,
+            [whole(column_mat.shape), w_block, whole(scale.shape), spec_whole],
+            [(spec_whole, full_shape), (pl.BlockSpec(grad_tile, at(0)), grad_shape)],
+            receive, None, grid=(channels // 2,),
+            scratch=[mix_scratch, *tiles_scratch], gated=True,
+        )
+
+    def grads(spec, other, held, first, count):
+        return pl.pallas_call(
+            partial(grads_rest_kernel, first=first),
+            grid=(count,),
+            in_specs=[spec_whole, spec_whole, pl.BlockSpec(memory_space=pl.ANY)],
+            out_specs=pl.BlockSpec(grad_tile, at(first)),
+            out_shape=grad_shape,
+            input_output_aliases={2: 0},
+            scratch_shapes=tiles_scratch,
+            compiler_params=params(),
+        )(spec, other, held)
+
+    values = over_y(to_rows(over_x(spectra), None, None))
+    mixed, forward_spec = mix(values, "gy")
+    back = from_rows(ring(mixed, "gy"), "gy", "gx")
+    hidden_spectra, hidden = route(
+        partial(slope_kernel, width=width), ring(back, "gx"),
+        [flat_field, cot_rows, point, table], spec_full, spec_full, spec_shape,
+        [whole(v.shape) for v in (flat_field, cot_rows, point, table)],
+        [(whole(flat_shape.shape), flat_shape)], "gx", "gx",
+        scratch=[pltpu.VMEM(flat_shape.shape, f32)],
+    )
+    values = to_rows(ring(hidden_spectra, "gx"), "gx", "gy")
+    mixed, hidden_spec, grad = mix_back(ring(values, "gy"), forward_spec, "gy")
+    first = channels // 2
+    middle = first + (block - first) * 5 // 14
+    grad = grads(forward_spec, hidden_spec, grad, first, middle - first)
+    back = from_rows(over_y(mixed), None, None)
+    grad_spectral = grads(forward_spec, hidden_spec, grad, middle, block - middle)
     back = over_x(back)
     grad_field = pl.pallas_call(
         partial(final_kernel, width=width),
-        grid=(tiles,),
-        in_specs=[
-            spec_block,
-            whole(flat_shape.shape),
-            pl.BlockSpec((channels * width, LANES), lambda c: (0, c)),
-            whole(table.shape),
-        ],
-        out_specs=cell_block,
         out_shape=shape((x_local, channels, y_local, cells), bf16),
         compiler_params=params(),
         name="final",

time: 221 us -> 203 us (0.919)
  blocking collectives: 76.7 us -> 12.7 us
  starting transfers between devices: 10.7 us -> 44.4 us
  waiting for transfers between devices: 11.5 us -> 28.3 us
  Pallas kernels: 117 us -> 109 us
  local copies, waits for them, and re-layouts: 2.34 us -> 5.06 us
    all_to_all x2 -> x0, blocking collectives: 38.7 us -> none  [over_x(): return lax.all_to_all(values, 'gx', 0, 0, tiled=True)]
    ppermute x0 -> x20, starting transfers between devices: none -> 27.9 us  [ring(): received[k] = lax.ppermute(blocks[k], axis, pairs)]
    all_to_all x3 -> x1, blocking collectives: 38 us -> 12.7 us  [over_y(): return lax.all_to_all(values, 'gy', 0, 0, tiled=True)]
    ppermute x0 -> x20, waiting for transfers between devices: none -> 15.2 us  [ring(): received[k] = lax.ppermute(blocks[k], axis, pairs)]
    pallas_call x11, Pallas kernels: 90.1 us -> 81.9 us  [the longest x7 51.2 us: route(): pl.pallas_call(body, grid=grid, in_specs=[pl.BlockSpec(memory_space=pltpu...]
    all_to_all x2, starting transfers between devices: 7.21 us -> 13 us  [over_x(): return lax.all_to_all(values, 'gx', 0, 0, tiled=True)]
    unnamed x6 -> x46, local copies, waits for them, and re-layouts: 2.34 us -> 5.06 us
  transfers between devices with their start and end apart: 3 -> 23, of which waited for: 1 -> 16; matrix products, arithmetic and copies ran while one was open for 0% -> 0% of each run, Pallas kernels for 28% -> 25%
where the time goes in v3:
time: 203 us; the launch traced here: 201 us
  Pallas kernels  109 us (54%)
  starting transfers between devices  44.4 us (22%)
  waiting for transfers between devices  28.3 us (14%)
  blocking collectives  12.7 us (6%)
  local copies, waits for them, and re-layouts  5.06 us (2%)
    pallas_call x7, Pallas kernels, route(): pl.pallas_call(body, grid=grid, in_specs=[pl.BlockSpec(memory_space=pltpu...  51.2 us
    ppermute x20, starting transfers between devices, ring(): received[k] = lax.ppermute(blocks[k], axis, pairs)  27.9 us
    pallas_call x2, Pallas kernels, grads(): pl.pallas_call(partial(grads_rest_kernel, first=first), grid=(count,), in...  22.4 us
    ppermute x20, waiting for transfers between devices, ring(): received[k] = lax.ppermute(blocks[k], axis, pairs)  15.2 us
    pallas_call x1, Pallas kernels, fused_device(): pl.pallas_call(pack_first_kernel, grid=(pack_head,), in_specs=[source], o...  14.7 us
    all_to_all x2, waiting for transfers between devices, over_x(): return lax.all_to_all(values, 'gx', 0, 0, tiled=True)  13.1 us
    all_to_all x2, starting transfers between devices, over_x(): return lax.all_to_all(values, 'gx', 0, 0, tiled=True)  13 us
    all_to_all x1, blocking collectives, over_y(): return lax.all_to_all(values, 'gy', 0, 0, tiled=True)  12.7 us
  transfers between devices with their start and end apart: 23, of which 16 were waited for; matrix products, arithmetic and copies ran while one was open for 0% of the time, Pallas kernels for 25%

profile of v3, /device:TPU:0, one launch (start us, length us, event | category | flops | bytes accessed | tf_op | source)
XLA Modules:
  0.0 201.2 jit_solution(15613058130149651675)
XLA Ops:
  0.6 3.1 %analyze.1 = (bf16[8,240,128]{2,1,0:T(8,128)(2,1)}, bf16[640,768]{1,0:T(8,128)(2,1)}) custom-call(bf16[4,20,8,768]{3,2,1,0:T(8,128)(2,1)} %bitcast.5, bf16[2,384,768]{2,1,0:T(8,128)(2,1)} %constant.17.clone.table_ref.refs_11_), custom_call_target="tpu_custom_call" | custom-call | tf_op jit(solution)/shard_map/analyze/pallas_call | solution.py:673
  3.7 7.3 %all-to-all-start = ((bf16[8,240,128]{2,1,0:T(8,128)(2,1)}), bf16[8,240,128]{2,1,0:T(8,128)(2,1)S(1)}, u32[]{:S(2)}, u32[]{:S(2)}) async-start(bf16[8,240,128]{2,1,0:T(8,128)(2,1)} %get-tuple-element.33), calls=%async_computation | async-start | bytes 983040 | tf_op jit(solution)/shard_map/all_to_all | solution.py:722
  11.0 0.7 pad_add_fusion.me_ref
  11.7 13.1 %all-to-all-done.refs_0_ = bf16[8,240,128]{2,1,0:T(8,128)(2,1)S(1)} async-done(((bf16[8,240,128]{2,1,0:T(8,128)(2,1)}), bf16[8,240,128]{2,1,0:T(8,128)(2,1)S(1)}, u32[]{:S(2)}, u32[]{:S(2)}) %all-to-all-start) | async-done | bytes 491552 | tf_op jit(solution)/shard_map/all_to_all | solution.py:722
  24.8 0.8 copy-done.1
  25.6 2.6 %shard_map.95 = f32[4,240,256]{2,1,0:T(8,128)} custom-call(s32[2]{0:T(128)} %pad_add_fusion.me_ref, bf16[8,240,128]{2,1,0:T(8,128)(2,1)} %copy-done.1, bf16[512,512]{1,0:T(8,128)(2,1)} %constant.18.clone.refs_1_.refs_4_.refs_8_), custom_call_target="tpu_custom_call" | custom-call | tf_op jit(solution)/shard_map/pallas_call | solution.py:649
  28.2 3.5 %all-to-all-start.1 = ((f32[4,240,256]{2,1,0:T(8,128)}), f32[4,240,256]{2,1,0:T(8,128)S(1)}, u32[]{:S(2)}, u32[]{:S(2)}) async-start(f32[4,240,256]{2,1,0:T(8,128)} %shard_map.95), calls=%async_computation.1 | async-start | bytes 1966080 | tf_op jit(solution)/shard_map/all_to_all | solution.py:725
  31.7 14.7 %pack_first.1._ = bf16[20,20,2,24,256]{4,3,2,1,0:T(8,128)(2,1)} custom-call(bf16[2,20,20,24,8,32]{5,4,3,2,1,0:T(8,128)(2,1)} %in_ref.3), custom_call_target="tpu_custom_call" | custom-call | tf_op jit(solution)/shard_map/pack_first/pallas_call | solution.py:693
  46.4 10.5 %pack_rest.1.refs_2_.refs_5_ = bf16[20,20,2,24,256]{4,3,2,1,0:T(8,128)(2,1)} custom-call(bf16[2,20,20,24,8,32]{5,4,3,2,1,0:T(8,128)(2,1)} %in_ref.3, bf16[20,20,2,24,256]{4,3,2,1,0:T(8,128)(2,1)} %pack_first.1._), custom_call_target="tpu_custom_call", output_to_operand_aliasing={{}: (1, {})} | custom-call | tf_op jit(solution)/shard_map/pack_rest/pallas_call | solution.py:703
  56.9 0.0 all-to-all-done.1.refs_0_
  56.9 0.9 copy-done
  57.8 11.8 %shard_map.96 = (bf16[240,256]{1,0:T(8,128)(2,1)}, bf16[240,256]{1,0:T(8,128)(2,1)}, bf16[240,256]{1,0:T(8,128)(2,1)}, bf16[240,256]{1,0:T(8,128)(2,1)}, f32[2,4,240,128]{3,2,1,0:T(8,128)}) custom-call(s32[2]{0:T(128)} %pad_add_fusion.me_ref, f32[4,240,256]{2,1,0:T(8,128)} %copy-done, bf16[512,512]{1,0:T(8,128)(2,1)} %constant.19.clone.refs_1_.refs_4_, ...), custom_call_target="tpu_custom_call" | custom-call | tf_op jit(solution)/shard_map/pallas_call | solution.py:649
  69.6 0.5 collective-permute-start
  70.0 1.6 collective-permute-start.1
  71.7 1.3 collective-permute-start.2
  73.0 1.4 collective-permute-done.refs_1_
  74.4 2.0 collective-permute-done.1.refs_2_
  76.3 1.3 collective-permute-done.2.refs_3_
  77.6 0.6 copy-done.8
  78.3 2.7 %shard_map.97 = (bf16[240,128]{1,0:T(8,128)(2,1)}, bf16[240,128]{1,0:T(8,128)(2,1)}, bf16[240,128]{1,0:T(8,128)(2,1)}, bf16[240,128]{1,0:T(8,128)(2,1)}, bf16[24...) custom-call(s32[2]{0:T(128)} %pad_add_fusion.me_ref, ...), custom_call_target="tpu_custom_call" | custom-call | tf_op jit(solution)/shard_map/pallas_call | solution.py:649
  81.0 1.5 collective-permute-start.3
  82.4 1.7 collective-permute-start.5
  84.2 2.9 %collective-permute-start.6 = (bf16[240,128]{1,0:T(8,128)(2,1)}, bf16[240,128]{1,0:T(8,128)(2,1)S(1)}, u32[]{:S(2)}, u32[]{:S(2)}) collective-permute-start(bf16[240,128]{1,0:T(8,128)(2,1)} %get-tuple-element.42), channel_id=1, source_target_pairs={{0,16},{4,20},{8,24},{12,28},{16,0},{20,4},{24,8},{28,12},{1,17},{... | collective-permute-start | bytes 184328 | tf_op jit(solution)/shard_map/ppermute | solution.py:667
  87.0 1.2 collective-permute-start.7
  88.3 0.6 collective-permute-done.3.refs_1_
  88.8 1.2 collective-permute-start.8
  90.1 0.8 collective-permute-start.9
  90.9 2.2 %point.1.refs_10_.point_ref = bf16[640,640]{1,0:T(8,128)(2,1)} custom-call(bf16[20,20]{1,0:T(8,128)(2,1)} %weight_ref.1), custom_call_target="tpu_custom_call" | custom-call | tf_op jit(solution)/shard_map/point/pallas_call | solution.py:714
  93.1 0.3 collective-permute-done.5.refs_3_
  93.4 0.4 collective-permute-done.6.refs_4_
  93.7 1.5 collective-permute-done.7.refs_5_
  95.2 0.1 collective-permute-done.8.refs_6_
  95.3 0.5 copy-done.13
  95.8 0.1 copy-done.14
  95.9 0.0 copy-done.15
  95.9 8.3 %shard_map.98 = (bf16[240,128]{1,0:T(8,128)(2,1)}, bf16[240,128]{1,0:T(8,128)(2,1)}, bf16[240,128]{1,0:T(8,128)(2,1)}, bf16[240,128]{1,0:T(8,128)(2,1)}, bf16[24...) custom-call(s32[2]{0:T(128)} %pad_add_fusion.me_ref, ...), custom_call_target="tpu_custom_call" | custom-call | tf_op jit(solution)/shard_map/pallas_call | solution.py:649
  104.3 2.1 %collective-permute-start.10 = (bf16[240,128]{1,0:T(8,128)(2,1)}, bf16[240,128]{1,0:T(8,128)(2,1)S(1)}, u32[]{:S(2)}, u32[]{:S(2)}) collective-permute-start(bf16[240,128]{1,0:T(8,128)(2,1)} %get-tuple-element.48), channel_id=1, source_target_pairs={{0,4},{4,8},{8,12},{12,16},{16,20},{20,24},{24,28},{28,0},{1,5},{5... | collective-permute-start | bytes 184328 | tf_op jit(solution)/shard_map/ppermute | solution.py:667
  106.4 2.1 %collective-permute-start.11 = (bf16[240,128]{1,0:T(8,128)(2,1)}, bf16[240,128]{1,0:T(8,128)(2,1)S(1)}, u32[]{:S(2)}, u32[]{:S(2)}) collective-permute-start(bf16[240,128]{1,0:T(8,128)(2,1)} %get-tuple-element.49), channel_id=1, source_target_pairs={{0,8},{4,12},{8,16},{12,20},{16,24},{20,28},{24,0},{28,4},{1,9},{5... | collective-permute-start | bytes 184328 | tf_op jit(solution)/shard_map/ppermute | solution.py:667
  108.5 0.7 collective-permute-start.12
  109.2 1.9 collective-permute-start.13
  111.1 2.5 %collective-permute-start.14 = (bf16[240,128]{1,0:T(8,128)(2,1)}, bf16[240,128]{1,0:T(8,128)(2,1)S(1)}, u32[]{:S(2)}, u32[]{:S(2)}) collective-permute-start(bf16[240,128]{1,0:T(8,128)(2,1)} %get-tuple-element.52), channel_id=1, source_target_pairs={{0,20},{4,24},{8,28},{12,0},{16,4},{20,8},{24,12},{28,16},{1,21},{... | collective-permute-start | bytes 184328 | tf_op jit(solution)/shard_map/ppermute | solution.py:667
  113.7 1.0 collective-permute-start.15
  114.7 1.5 collective-permute-start.16
  116.3 0.8 collective-permute-done.12.refs_3_
  117.0 1.1 collective-permute-done.13.refs_4_
  118.1 0.5 collective-permute-done.14.refs_5_
  118.6 0.8 collective-permute-done.15.refs_6_
  119.5 0.6 copy-done.21
  120.1 0.0 copy-done.22
  120.1 2.7 %shard_map.99 = (bf16[240,256]{1,0:T(8,128)(2,1)}, bf16[240,256]{1,0:T(8,128)(2,1)}, bf16[240,256]{1,0:T(8,128)(2,1)}, bf16[240,256]{1,0:T(8,128)(2,1)}) custom-call(s32[2]{0:T(128)} %pad_add_fusion.me_ref, bf16[240,128]{1,0:T(8,128)(2,1)} %get-tuple-element.47.refs_0_, bf16[240,128]{1,0:T(8,128)(2,1)} %copy-done.16, bf16[240,128]{1,0:T(8,128)(2,1)} %copy-done.17, ...), custom_call_target="tpu_custom_call" | custom-call | tf_op jit(solution)/shard_map/pallas_call | solution.py:649
  122.8 1.7 collective-permute-start.18
  124.5 1.4 collective-permute-start.19
  125.9 2.1 %collective-permute-done.17.refs_1_ = bf16[240,256]{1,0:T(8,128)(2,1)S(1)} collective-permute-done((bf16[240,256]{1,0:T(8,128)(2,1)}, bf16[240,256]{1,0:T(8,128)(2,1)S(1)}, u32[]{:S(2)}, u32[]{:S(2)}) %collective-permute-start.17) | collective-permute-done | bytes 122912 | tf_op jit(solution)/shard_map/ppermute | solution.py:667
  128.0 1.3 collective-permute-done.18.refs_2_
  129.2 1.3 collective-permute-done.19.refs_3_
  130.5 0.6 copy-done.5
  131.2 20.6 %shard_map.100 = (bf16[4,240,256]{2,1,0:T(8,128)(2,1)}, f32[2,4,240,128]{3,2,1,0:T(8,128)}, f32[2,20,20,24,8,32]{5,4,3,2,1,0:T(8,128)}) custom-call(s32[2]{0:T(128)} %pad_add_fusion.me_ref, bf16[240,256]{1,0:T(8,128)(2,1)} %get-tuple-element.55.refs_0_, bf16[240,256]{1,0:T(8,128)(2,1)} %copy-done.3, bf16[240,256]{1,0:T(8,128)(2,1)} %copy-done.4, ...), custom_call_target="tpu_custom_call" | custom-call | tf_op jit(solution)/shard_map/pallas_call | solution.py:649
  151.8 12.7 %all_to_all.20.refs_0_ = bf16[4,240,256]{2,1,0:T(8,128)(2,1)} all-to-all(bf16[4,240,256]{2,1,0:T(8,128)(2,1)} %get-tuple-element.60), channel_id=1, replica_groups=mesh['gx'=8,'gy'=4] {'gy'}, dimensions={0} | all-to-all | bytes 983040 | tf_op jit(solution)/shard_map/all_to_all | solution.py:725
  164.5 2.6 %shard_map.101 = bf16[8,240,128]{2,1,0:T(8,128)(2,1)} custom-call(s32[2]{0:T(128)} %pad_add_fusion.me_ref, bf16[4,240,256]{2,1,0:T(8,128)(2,1)} %all_to_all.20.refs_0_, bf16[512,512]{1,0:T(8,128)(2,1)} %constant.18.clone.refs_1_.refs_4_.refs_8_), custom_call_target="tpu_custom_call" | custom-call | tf_op jit(solution)/shard_map/pallas_call | solution.py:649
  167.1 5.7 %all-to-all-start.3 = ((bf16[8,240,128]{2,1,0:T(8,128)(2,1)}), bf16[8,240,128]{2,1,0:T(8,128)(2,1)S(1)}, u32[]{:S(2)}, u32[]{:S(2)}) async-start(bf16[8,240,128]{2,1,0:T(8,128)(2,1)} %shard_map.101), calls=%async_computation.3 | async-start | bytes 983040 | tf_op jit(solution)/shard_map/all_to_all | solution.py:722
  172.8 8.8 %shard_map.102._ = f32[2,20,20,24,8,32]{5,4,3,2,1,0:T(8,128)} custom-call(f32[2,4,240,128]{3,2,1,0:T(8,128)} %get-tuple-element.59.refs_7_.f_spec_ref, f32[2,4,240,128]{3,2,1,0:T(8,128)} %get-tuple-element.62.h_spec_ref, f32[2,20,20,24,8,32]{5,4,3,2,1,0:T(8,128)} %get-tuple-element.63._), custom_call_target="tpu_custom_call", output_to_operand_aliasing={{}: (2, {})} | custom-call | tf_op jit(solution)/shard_map/pallas_call | solution.py:773
  181.6 13.6 %shard_map.103 = f32[2,20,20,24,8,32]{5,4,3,2,1,0:T(8,128)} custom-call(f32[2,4,240,128]{3,2,1,0:T(8,128)} %get-tuple-element.59.refs_7_.f_spec_ref, f32[2,4,240,128]{3,2,1,0:T(8,128)} %get-tuple-element.62.h_spec_ref, f32[2,20,20,24,8,32]{5,4,3,2,1,0:T(8,128)} %shard_map.102._), custom_call_target="tpu_custom_call", output_to_operand_aliasing={{}: (2, {})} | custom-call | tf_op jit(solution)/shard_map/pallas_call | solution.py:773
  195.2 0.8 copy-done.2
  196.0 5.2 %final.1 = bf16[4,20,8,768]{3,2,1,0:T(8,128)(2,1)} custom-call(bf16[8,240,128]{2,1,0:T(8,128)(2,1)} %copy-done.2, bf16[640,768]{1,0:T(8,128)(2,1)} %get-tuple-element.61.hidden_ref, bf16[640,640]{1,0:T(8,128)(2,1)} %point.1.refs_10_.point_ref, bf16[2,384,768]{2,1,0:T(8,128)(2,1)} %constant.17.clone.table_ref.refs_11_), custom_call_target="tpu_custom_call" | custom-call | tf_op jit(solution)/shard_map/final/pallas_call | solution.py:802
  (44 shorter events, 0.1 us)
Async XLA Ops:
  3.7 21.1 %all-to-all-start = ((bf16[8,240,128]{2,1,0:T(8,128)(2,1)}), bf16[8,240,128]{2,1,0:T(8,128)(2,1)S(1)}, u32[]{:S(2)}, u32[]{:S(2)}) async-start(bf16[8,240,128]{2,1,0:T(8,128)(2,1)} %get-tuple-element.33), calls=%async_computation | async-start | bytes 983040 | tf_op jit(solution)/shard_map/all_to_all | solution.py:722
  24.8 0.8 copy-start.1
  28.2 28.7 %all-to-all-start.1 = ((f32[4,240,256]{2,1,0:T(8,128)}), f32[4,240,256]{2,1,0:T(8,128)S(1)}, u32[]{:S(2)}, u32[]{:S(2)}) async-start(f32[4,240,256]{2,1,0:T(8,128)} %shard_map.95), calls=%async_computation.1 | async-start | bytes 1966080 | tf_op jit(solution)/shard_map/all_to_all | solution.py:725
  56.9 0.9 copy-start
  69.6 4.8 %collective-permute-start = (bf16[240,256]{1,0:T(8,128)(2,1)}, bf16[240,256]{1,0:T(8,128)(2,1)S(1)}, u32[]{:S(2)}, u32[]{:S(2)}) collective-permute-start(bf16[240,256]{1,0:T(8,128)(2,1)} %get-tuple-element.35), channel_id=1, source_target_pairs={{0,1},{1,2},{2,3},{3,0},{4,5},{5,6},{6,7},{7,4},{8,9},{9,10},{10,1... | collective-permute-start | bytes 368648 | tf_op jit(solution)/shard_map/ppermute | solution.py:667
  70.0 6.3 %collective-permute-start.1 = (bf16[240,256]{1,0:T(8,128)(2,1)}, bf16[240,256]{1,0:T(8,128)(2,1)S(1)}, u32[]{:S(2)}, u32[]{:S(2)}) collective-permute-start(bf16[240,256]{1,0:T(8,128)(2,1)} %get-tuple-element.36), channel_id=1, source_target_pairs={{0,2},{1,3},{2,0},{3,1},{4,6},{5,7},{6,4},{7,5},{8,10},{9,11},{10,... | collective-permute-start | bytes 368648 | tf_op jit(solution)/shard_map/ppermute | solution.py:667
  71.7 6.0 %collective-permute-start.2 = (bf16[240,256]{1,0:T(8,128)(2,1)}, bf16[240,256]{1,0:T(8,128)(2,1)S(1)}, u32[]{:S(2)}, u32[]{:S(2)}) collective-permute-start(bf16[240,256]{1,0:T(8,128)(2,1)} %get-tuple-element.37), channel_id=1, source_target_pairs={{0,3},{1,0},{2,1},{3,2},{4,7},{5,4},{6,5},{7,6},{8,11},{9,8},{10,9... | collective-permute-start | bytes 368648 | tf_op jit(solution)/shard_map/ppermute | solution.py:667
  74.4 3.3 %copy-start.6 = (bf16[240,256]{1,0:T(8,128)(2,1)}, bf16[240,256]{1,0:T(8,128)(2,1)S(1)}, u32[]{:S(2)}) copy-start(bf16[240,256]{1,0:T(8,128)(2,1)S(1)} %collective-permute-done.refs_1_) | copy-start | bytes 368644
  76.3 1.3 copy-start.7
  77.6 0.6 copy-start.8
  81.0 7.9 %collective-permute-start.3 = (bf16[240,128]{1,0:T(8,128)(2,1)}, bf16[240,128]{1,0:T(8,128)(2,1)S(1)}, u32[]{:S(2)}, u32[]{:S(2)}) collective-permute-start(bf16[240,128]{1,0:T(8,128)(2,1)} %get-tuple-element.39), channel_id=1, source_target_pairs={{0,4},{4,8},{8,12},{12,16},{16,20},{20,24},{24,28},{28,0},{1,5},{5... | collective-permute-start | bytes 184328 | tf_op jit(solution)/shard_map/ppermute | solution.py:667
  82.4 7.7 %collective-permute-start.4 = (bf16[240,128]{1,0:T(8,128)(2,1)}, bf16[240,128]{1,0:T(8,128)(2,1)S(1)}, u32[]{:S(2)}, u32[]{:S(2)}) collective-permute-start(bf16[240,128]{1,0:T(8,128)(2,1)} %get-tuple-element.40), channel_id=1, source_target_pairs={{0,8},{4,12},{8,16},{12,20},{16,24},{20,28},{24,0},{28,4},{1,9},{5... | collective-permute-start | bytes 184328 | tf_op jit(solution)/shard_map/ppermute | solution.py:667
  82.4 10.9 %collective-permute-start.5 = (bf16[240,128]{1,0:T(8,128)(2,1)}, bf16[240,128]{1,0:T(8,128)(2,1)S(1)}, u32[]{:S(2)}, u32[]{:S(2)}) collective-permute-start(bf16[240,128]{1,0:T(8,128)(2,1)} %get-tuple-element.41), channel_id=1, source_target_pairs={{0,12},{4,16},{8,20},{12,24},{16,28},{20,0},{24,4},{28,8},{1,13},{... | collective-permute-start | bytes 184328 | tf_op jit(solution)/shard_map/ppermute | solution.py:667
  84.2 9.6 %collective-permute-start.6 = (bf16[240,128]{1,0:T(8,128)(2,1)}, bf16[240,128]{1,0:T(8,128)(2,1)S(1)}, u32[]{:S(2)}, u32[]{:S(2)}) collective-permute-start(bf16[240,128]{1,0:T(8,128)(2,1)} %get-tuple-element.42), channel_id=1, source_target_pairs={{0,16},{4,20},{8,24},{12,28},{16,0},{20,4},{24,8},{28,12},{1,17},{... | collective-permute-start | bytes 184328 | tf_op jit(solution)/shard_map/ppermute | solution.py:667
  87.0 8.2 %collective-permute-start.7 = (bf16[240,128]{1,0:T(8,128)(2,1)}, bf16[240,128]{1,0:T(8,128)(2,1)S(1)}, u32[]{:S(2)}, u32[]{:S(2)}) collective-permute-start(bf16[240,128]{1,0:T(8,128)(2,1)} %get-tuple-element.43), channel_id=1, source_target_pairs={{0,20},{4,24},{8,28},{12,0},{16,4},{20,8},{24,12},{28,16},{1,21},{... | collective-permute-start | bytes 184328 | tf_op jit(solution)/shard_map/ppermute | solution.py:667
  88.8 6.5 %copy-start.9 = (bf16[240,128]{1,0:T(8,128)(2,1)}, bf16[240,128]{1,0:T(8,128)(2,1)S(1)}, u32[]{:S(2)}) copy-start(bf16[240,128]{1,0:T(8,128)(2,1)S(1)} %collective-permute-done.3.refs_1_) | copy-start | bytes 184324
  88.8 6.5 %collective-permute-start.8 = (bf16[240,128]{1,0:T(8,128)(2,1)}, bf16[240,128]{1,0:T(8,128)(2,1)S(1)}, u32[]{:S(2)}, u32[]{:S(2)}) collective-permute-start(bf16[240,128]{1,0:T(8,128)(2,1)} %get-tuple-element.44), channel_id=1, source_target_pairs={{0,24},{4,28},{8,0},{12,4},{16,8},{20,12},{24,16},{28,20},{1,25},{... | collective-permute-start | bytes 184328 | tf_op jit(solution)/shard_map/ppermute | solution.py:667
  90.1 5.2 %copy-start.10 = (bf16[240,128]{1,0:T(8,128)(2,1)}, bf16[240,128]{1,0:T(8,128)(2,1)S(1)}, u32[]{:S(2)}) copy-start(bf16[240,128]{1,0:T(8,128)(2,1)S(1)} %collective-permute-done.4.refs_2_) | copy-start | bytes 184324
  90.1 5.2 %collective-permute-start.9 = (bf16[240,128]{1,0:T(8,128)(2,1)}, bf16[240,128]{1,0:T(8,128)(2,1)S(1)}, u32[]{:S(2)}, u32[]{:S(2)}) collective-permute-start(bf16[240,128]{1,0:T(8,128)(2,1)} %get-tuple-element.45), channel_id=1, source_target_pairs={{0,28},{4,0},{8,4},{12,8},{16,12},{20,16},{24,20},{28,24},{1,29},{... | collective-permute-start | bytes 184328 | tf_op jit(solution)/shard_map/ppermute | solution.py:667
  93.4 2.0 copy-start.11
  93.7 1.6 copy-start.12
  95.2 0.6 copy-start.13
  95.3 0.6 copy-start.14
  95.3 0.6 copy-start.15
  104.3 9.4 %collective-permute-start.10 = (bf16[240,128]{1,0:T(8,128)(2,1)}, bf16[240,128]{1,0:T(8,128)(2,1)S(1)}, u32[]{:S(2)}, u32[]{:S(2)}) collective-permute-start(bf16[240,128]{1,0:T(8,128)(2,1)} %get-tuple-element.48), channel_id=1, source_target_pairs={{0,4},{4,8},{8,12},{12,16},{16,20},{20,24},{24,28},{28,0},{1,5},{5... | collective-permute-start | bytes 184328 | tf_op jit(solution)/shard_map/ppermute | solution.py:667
  106.4 8.3 %collective-permute-start.11 = (bf16[240,128]{1,0:T(8,128)(2,1)}, bf16[240,128]{1,0:T(8,128)(2,1)S(1)}, u32[]{:S(2)}, u32[]{:S(2)}) collective-permute-start(bf16[240,128]{1,0:T(8,128)(2,1)} %get-tuple-element.49), channel_id=1, source_target_pairs={{0,8},{4,12},{8,16},{12,20},{16,24},{20,28},{24,0},{28,4},{1,9},{5... | collective-permute-start | bytes 184328 | tf_op jit(solution)/shard_map/ppermute | solution.py:667
  108.5 8.5 %collective-permute-start.12 = (bf16[240,128]{1,0:T(8,128)(2,1)}, bf16[240,128]{1,0:T(8,128)(2,1)S(1)}, u32[]{:S(2)}, u32[]{:S(2)}) collective-permute-start(bf16[240,128]{1,0:T(8,128)(2,1)} %get-tuple-element.50), channel_id=1, source_target_pairs={{0,12},{4,16},{8,20},{12,24},{16,28},{20,0},{24,4},{28,8},{1,13},{... | collective-permute-start | bytes 184328 | tf_op jit(solution)/shard_map/ppermute | solution.py:667
  109.2 8.9 %collective-permute-start.13 = (bf16[240,128]{1,0:T(8,128)(2,1)}, bf16[240,128]{1,0:T(8,128)(2,1)S(1)}, u32[]{:S(2)}, u32[]{:S(2)}) collective-permute-start(bf16[240,128]{1,0:T(8,128)(2,1)} %get-tuple-element.51), channel_id=1, source_target_pairs={{0,16},{4,20},{8,24},{12,28},{16,0},{20,4},{24,8},{28,12},{1,17},{... | collective-permute-start | bytes 184328 | tf_op jit(solution)/shard_map/ppermute | solution.py:667
  111.1 7.5 %collective-permute-start.14 = (bf16[240,128]{1,0:T(8,128)(2,1)}, bf16[240,128]{1,0:T(8,128)(2,1)S(1)}, u32[]{:S(2)}, u32[]{:S(2)}) collective-permute-start(bf16[240,128]{1,0:T(8,128)(2,1)} %get-tuple-element.52), channel_id=1, source_target_pairs={{0,20},{4,24},{8,28},{12,0},{16,4},{20,8},{24,12},{28,16},{1,21},{... | collective-permute-start | bytes 184328 | tf_op jit(solution)/shard_map/ppermute | solution.py:667
  113.7 5.8 %copy-start.16 = (bf16[240,128]{1,0:T(8,128)(2,1)}, bf16[240,128]{1,0:T(8,128)(2,1)S(1)}, u32[]{:S(2)}) copy-start(bf16[240,128]{1,0:T(8,128)(2,1)S(1)} %collective-permute-done.10.refs_1_) | copy-start | bytes 184324
  113.7 5.7 %collective-permute-start.15 = (bf16[240,128]{1,0:T(8,128)(2,1)}, bf16[240,128]{1,0:T(8,128)(2,1)S(1)}, u32[]{:S(2)}, u32[]{:S(2)}) collective-permute-start(bf16[240,128]{1,0:T(8,128)(2,1)} %get-tuple-element.53), channel_id=1, source_target_pairs={{0,24},{4,28},{8,0},{12,4},{16,8},{20,12},{24,16},{28,20},{1,25},{... | collective-permute-start | bytes 184328 | tf_op jit(solution)/shard_map/ppermute | solution.py:667
  114.7 4.7 %copy-start.17 = (bf16[240,128]{1,0:T(8,128)(2,1)}, bf16[240,128]{1,0:T(8,128)(2,1)S(1)}, u32[]{:S(2)}) copy-start(bf16[240,128]{1,0:T(8,128)(2,1)S(1)} %collective-permute-done.11.refs_2_) | copy-start | bytes 184324
  114.7 4.7 %collective-permute-start.16 = (bf16[240,128]{1,0:T(8,128)(2,1)}, bf16[240,128]{1,0:T(8,128)(2,1)S(1)}, u32[]{:S(2)}, u32[]{:S(2)}) collective-permute-start(bf16[240,128]{1,0:T(8,128)(2,1)} %get-tuple-element.54), channel_id=1, source_target_pairs={{0,28},{4,0},{8,4},{12,8},{16,12},{20,16},{24,20},{28,24},{1,29},{... | collective-permute-start | bytes 184328 | tf_op jit(solution)/shard_map/ppermute | solution.py:667
  117.0 2.4 %copy-start.18 = (bf16[240,128]{1,0:T(8,128)(2,1)}, bf16[240,128]{1,0:T(8,128)(2,1)S(1)}, u32[]{:S(2)}) copy-start(bf16[240,128]{1,0:T(8,128)(2,1)S(1)} %collective-permute-done.12.refs_3_) | copy-start | bytes 184324
  118.1 1.4 copy-start.19
  118.6 0.9 copy-start.20
  119.4 0.6 copy-start.21
  119.4 0.6 copy-start.22
  122.8 5.2 %collective-permute-start.17 = (bf16[240,256]{1,0:T(8,128)(2,1)}, bf16[240,256]{1,0:T(8,128)(2,1)S(1)}, u32[]{:S(2)}, u32[]{:S(2)}) collective-permute-start(bf16[240,256]{1,0:T(8,128)(2,1)} %get-tuple-element.56), channel_id=1, source_target_pairs={{0,1},{1,2},{2,3},{3,0},{4,5},{5,6},{6,7},{7,4},{8,9},{9,10},{10,1... | collective-permute-start | bytes 368648 | tf_op jit(solution)/shard_map/ppermute | solution.py:667
  122.8 6.5 %collective-permute-start.18 = (bf16[240,256]{1,0:T(8,128)(2,1)}, bf16[240,256]{1,0:T(8,128)(2,1)S(1)}, u32[]{:S(2)}, u32[]{:S(2)}) collective-permute-start(bf16[240,256]{1,0:T(8,128)(2,1)} %get-tuple-element.57), channel_id=1, source_target_pairs={{0,2},{1,3},{2,0},{3,1},{4,6},{5,7},{6,4},{7,5},{8,10},{9,11},{10,... | collective-permute-start | bytes 368648 | tf_op jit(solution)/shard_map/ppermute | solution.py:667
  124.5 6.0 %collective-permute-start.19 = (bf16[240,256]{1,0:T(8,128)(2,1)}, bf16[240,256]{1,0:T(8,128)(2,1)S(1)}, u32[]{:S(2)}, u32[]{:S(2)}) collective-permute-start(bf16[240,256]{1,0:T(8,128)(2,1)} %get-tuple-element.58), channel_id=1, source_target_pairs={{0,3},{1,0},{2,1},{3,2},{4,7},{5,4},{6,5},{7,6},{8,11},{9,8},{10,9... | collective-permute-start | bytes 368648 | tf_op jit(solution)/shard_map/ppermute | solution.py:667
  128.0 2.6 %copy-start.3 = (bf16[240,256]{1,0:T(8,128)(2,1)}, bf16[240,256]{1,0:T(8,128)(2,1)S(1)}, u32[]{:S(2)}) copy-start(bf16[240,256]{1,0:T(8,128)(2,1)S(1)} %collective-permute-done.17.refs_1_) | copy-start | bytes 368644
  129.2 1.3 copy-start.4
  130.5 0.7 copy-start.5
  167.1 28.1 %all-to-all-start.3 = ((bf16[8,240,128]{2,1,0:T(8,128)(2,1)}), bf16[8,240,128]{2,1,0:T(8,128)(2,1)S(1)}, u32[]{:S(2)}, u32[]{:S(2)}) async-start(bf16[8,240,128]{2,1,0:T(8,128)(2,1)} %shard_map.101), calls=%async_computation.3 | async-start | bytes 983040 | tf_op jit(solution)/shard_map/all_to_all | solution.py:722
  195.2 0.8 copy-start.2

commit v4 on v3

--- a/solution.py
+++ b/solution.py
@@ -492,9 +492,11 @@
 
 
 def pack_body(in_ref, out_ref):
-    for i in range(in_ref.shape[1]):
-        for p in range(2):
-            out_ref[i, :, p] = pltpu.einshape("omky->om(ky)", in_ref[p, i])
+    def step(n, carry):
+        out_ref[n // 2, :, n % 2] = pltpu.einshape("omky->om(ky)", in_ref[n % 2, n // 2])
+        return carry
+
+    lax.fori_loop(0, 2 * in_ref.shape[1], step, 0)
 
 
 def pack_first_kernel(in_ref, out_ref):
@@ -605,7 +607,7 @@
     plane = kx_local * ky
     bf16, f32 = jnp.bfloat16, jnp.float32
     shape = jax.ShapeDtypeStruct
-    params = partial(pltpu.CompilerParams, vmem_limit_bytes=58 * 1024 * 1024)
+    params = partial(pltpu.CompilerParams, vmem_limit_bytes=28 * 1024 * 1024)
 
     table = jnp.asarray(cell_table())
     row_mat = jnp.asarray(row_table(groups_x, x_local, y_local, groups_y))
@@ -613,8 +615,8 @@
     scale = jnp.asarray(scale_table(block, LANES, cell_total))
 
     spec_shape = shape((groups_x, rows, LANES), bf16)
-    flat_shape = shape((channels * width, cells), bf16)
-    full_shape = shape((2, 2 * plane // LANES, rows, LANES), f32)
+    flat_shape = pltpu.HBM((channels * width, cells), bf16)
+    full_shape = pltpu.HBM((2, 2 * plane // LANES, rows, LANES), f32)
     mid_shape = shape((groups_y, rows, 2 * lanes), bf16)
 
     me = jnp.stack([lax.axis_index("gx"), lax.axis_index("gy")]).astype(jnp.int32)
@@ -667,8 +669,12 @@
             received[k] = lax.ppermute(blocks[k], axis, pairs)
         return received
 
-    field_rows = field.transpose(0, 2, 1, 3)
-    cot_rows = cotangent.transpose(0, 2, 1, 3)
+    def resident(values):
+        return pltpu.with_memory_space_constraint(values, pltpu.HBM)
+
+    field_rows = resident(field.transpose(0, 2, 1, 3))
+    cot_rows = resident(cotangent.transpose(0, 2, 1, 3))
+    table, row_mat, column_mat = resident(table), resident(row_mat), resident(column_mat)
 
     spectra, flat_field = pl.pallas_call(
         partial(analyze_kernel, width=width),
@@ -677,7 +683,7 @@
         name="analyze",
     )(field_rows, table)
 
-    pack_shape = shape((channels, channels, 2, block, plane), bf16)
+    pack_shape = pltpu.HBM((channels, channels, 2, block, plane), bf16)
     pack_steps = channels // 2
     pack_head = pack_steps * 3 // 5
 
@@ -703,13 +709,14 @@
     packed = pl.pallas_call(
         pack_rest_kernel,
         grid=(pack_steps - pack_head,),
-        in_specs=[source, pl.BlockSpec(memory_space=pl.ANY)],
+        in_specs=[source, pl.BlockSpec(memory_space=pltpu.HBM)],
         out_specs=target,
         out_shape=pack_shape,
         input_output_aliases={1: 0},
         compiler_params=params(),
         name="pack_rest",
     )(weight, packed)
+    packed = resident(packed)
 
     point = pl.pallas_call(
         partial(point_kernel, width=width),
@@ -740,7 +747,7 @@
         )[0]
 
     grad_tile = (2, channels, channels, 1, kx_local, ky)
-    grad_shape = shape((2, channels, channels, block, kx_local, ky), f32)
+    grad_shape = pltpu.HBM((2, channels, channels, block, kx_local, ky), f32)
     tiles_scratch = [pltpu.VMEM((2, 2, channels // 2 * kx_local, LANES), f32)] * 2
     mix_scratch = pltpu.VMEM((2, rows, 2 * plane), f32)
     spec_whole = whole(full_shape.shape)
@@ -784,6 +791,7 @@
     values = over_y(to_rows(over_x(spectra), None, None))
     mixed, forward_spec = mix(values, "gy")
     back = from_rows(ring(mixed, "gy"), "gy", "gx")
+    flat_field = resident(flat_field)
     hidden_spectra, hidden = route(
         partial(slope_kernel, width=width), ring(back, "gx"),
         [flat_field, cot_rows, point, table], spec_full, spec_full, spec_shape,
@@ -792,7 +800,9 @@
         scratch=[pltpu.VMEM(flat_shape.shape, f32)],
     )
     values = to_rows(ring(hidden_spectra, "gx"), "gx", "gy")
+    forward_spec = resident(forward_spec)
     mixed, hidden_spec, grad = mix_back(ring(values, "gy"), forward_spec, "gy")
+    hidden, forward_spec, hidden_spec = map(resident, (hidden, forward_spec, hidden_spec))
     first = channels // 2
     middle = first + (block - first) * 5 // 14
     grad = grads(forward_spec, hidden_spec, grad, first, middle - first)

time: 203 us -> 192 us (0.946)
  local copies, waits for them, and re-layouts: 5.06 us -> 0.01 us
  Pallas kernels: 109 us -> 104 us
    unnamed x46 -> x4, local copies, waits for them, and re-layouts: 5.06 us -> 0.01 us
    pallas_call x7, Pallas kernels: 51.2 us -> 47.2 us  [route(): pl.pallas_call(body, grid=grid, in_specs=[pl.BlockSpec(memory_space=pltpu...]
  transfers between devices with their start and end apart: 23 -> 23, of which waited for: 16 -> 16; matrix products, arithmetic and copies ran while one was open for 0% -> 0% of each run, Pallas kernels for 25% -> 26%
where the time goes in v4:
time: 192 us; the launch traced here: 191 us
  Pallas kernels  104 us (54%)
  starting transfers between devices  44.5 us (23%)
  waiting for transfers between devices  29.5 us (15%)
  blocking collectives  11.4 us (6%)
    pallas_call x7, Pallas kernels, route(): pl.pallas_call(body, grid=grid, in_specs=[pl.BlockSpec(memory_space=pltpu...  47.2 us
    ppermute x20, starting transfers between devices, ring(): received[k] = lax.ppermute(blocks[k], axis, pairs)  28 us
    pallas_call x2, Pallas kernels, grads(): pl.pallas_call(partial(grads_rest_kernel, first=first), grid=(count,), in...  22.4 us
    ppermute x20, waiting for transfers between devices, ring(): received[k] = lax.ppermute(blocks[k], axis, pairs)  15.8 us
    pallas_call x1, Pallas kernels, fused_device(): pl.pallas_call(pack_first_kernel, grid=(pack_head,), in_specs=[source], o...  15.4 us
    all_to_all x2, waiting for transfers between devices, over_x(): return lax.all_to_all(values, 'gx', 0, 0, tiled=True)  13.7 us
    all_to_all x2, starting transfers between devices, over_x(): return lax.all_to_all(values, 'gx', 0, 0, tiled=True)  13 us
    all_to_all x1, blocking collectives, over_y(): return lax.all_to_all(values, 'gy', 0, 0, tiled=True)  11.4 us
  transfers between devices with their start and end apart: 23, of which 16 were waited for; matrix products, arithmetic and copies ran while one was open for 0% of the time, Pallas kernels for 26%

profile of v4, /device:TPU:0, one launch (start us, length us, event | category | flops | bytes accessed | tf_op | source)
XLA Modules:
  0.0 190.5 jit_solution(8905745670926202200)
XLA Ops:
  0.6 3.1 %analyze.1 = (bf16[8,240,128]{2,1,0:T(8,128)(2,1)}, bf16[640,768]{1,0:T(8,128)(2,1)}) custom-call(bf16[4,20,8,768]{3,2,1,0:T(8,128)(2,1)} %bitcast.5, bf16[2,384,768]{2,1,0:T(8,128)(2,1)} %constant.17.clone.table_ref.refs_11_), custom_call_target="tpu_custom_call" | custom-call | tf_op jit(solution)/shard_map/analyze/pallas_call | solution.py:679
  3.7 7.3 %all-to-all-start = ((bf16[8,240,128]{2,1,0:T(8,128)(2,1)}), bf16[8,240,128]{2,1,0:T(8,128)(2,1)S(1)}, u32[]{:S(2)}, u32[]{:S(2)}) async-start(bf16[8,240,128]{2,1,0:T(8,128)(2,1)} %get-tuple-element.33), calls=%async_computation | async-start | bytes 983040 | tf_op jit(solution)/shard_map/all_to_all | solution.py:729
  11.0 0.1 pad_add_fusion.me_ref
  11.1 13.7 %all-to-all-done.refs_0_ = bf16[8,240,128]{2,1,0:T(8,128)(2,1)S(1)} async-done(((bf16[8,240,128]{2,1,0:T(8,128)(2,1)}), bf16[8,240,128]{2,1,0:T(8,128)(2,1)S(1)}, u32[]{:S(2)}, u32[]{:S(2)}) %all-to-all-start) | async-done | bytes 491552 | tf_op jit(solution)/shard_map/all_to_all | solution.py:729
  24.8 2.5 %shard_map.95 = f32[4,240,256]{2,1,0:T(8,128)} custom-call(s32[2]{0:T(128)S(1)} %pad_add_fusion.me_ref, bf16[8,240,128]{2,1,0:T(8,128)(2,1)S(1)} %all-to-all-done.refs_0_, bf16[512,512]{1,0:T(8,128)(2,1)} %constant.18.clone.refs_1_.refs_4_.refs_8_), custom_call_target="tpu_custom_call" | custom-call | tf_op jit(solution)/shard_map/pallas_call | solution.py:651
  27.3 3.5 %all-to-all-start.1 = ((f32[4,240,256]{2,1,0:T(8,128)}), f32[4,240,256]{2,1,0:T(8,128)S(1)}, u32[]{:S(2)}, u32[]{:S(2)}) async-start(f32[4,240,256]{2,1,0:T(8,128)} %shard_map.95), calls=%async_computation.1 | async-start | bytes 1966080 | tf_op jit(solution)/shard_map/all_to_all | solution.py:732
  30.8 15.4 %pack_first.1._ = bf16[20,20,2,24,256]{4,3,2,1,0:T(8,128)(2,1)} custom-call(bf16[2,20,20,24,8,32]{5,4,3,2,1,0:T(8,128)(2,1)} %in_ref.3), custom_call_target="tpu_custom_call" | custom-call | tf_op jit(solution)/shard_map/pack_first/pallas_call | solution.py:699
  46.1 11.0 %pack_rest.1.refs_2_.refs_5_ = bf16[20,20,2,24,256]{4,3,2,1,0:T(8,128)(2,1)} custom-call(bf16[2,20,20,24,8,32]{5,4,3,2,1,0:T(8,128)(2,1)} %in_ref.3, bf16[20,20,2,24,256]{4,3,2,1,0:T(8,128)(2,1)} %pack_first.1._), custom_call_target="tpu_custom_call", output_to_operand_aliasing={{}: (1, {})} | custom-call | tf_op jit(solution)/shard_map/pack_rest/pallas_call | solution.py:709
  57.1 0.0 all-to-all-done.1.refs_0_
  57.1 0.0 copy-done
  57.1 11.2 %shard_map.96 = (bf16[240,256]{1,0:T(8,128)(2,1)S(1)}, bf16[240,256]{1,0:T(8,128)(2,1)S(1)}, bf16[240,256]{1,0:T(8,128)(2,1)S(1)}, bf16[240,256]{1,0:T(8,128)(2,1)S(1)}, f32[2,4,240,128]{3,2,1,0:T(8,128)}) custom-call(s32[2]{0:T(128)S(1)} %pad_add_fusion.me_ref, f32[4,240,256]{2,1,0:T(8,128)S(1)} %all-to-all-done.1.refs_0_, ...), custom_call_target="tpu_custom_call" | custom-call | tf_op jit(solution)/shard_map/pallas_call | solution.py:651
  68.3 0.5 collective-permute-start
  68.7 1.6 collective-permute-start.1
  70.4 1.3 collective-permute-start.2
  71.7 1.1 collective-permute-done.refs_1_
  72.9 2.0 %collective-permute-done.1.refs_2_ = bf16[240,256]{1,0:T(8,128)(2,1)S(1)} collective-permute-done((bf16[240,256]{1,0:T(8,128)(2,1)S(1)}, bf16[240,256]{1,0:T(8,128)(2,1)S(1)}, u32[]{:S(2)}, u32[]{:S(2)}) %collective-permute-start.1) | collective-permute-done | bytes 122912 | tf_op jit(solution)/shard_map/ppermute | solution.py:669
  74.8 1.2 collective-permute-done.2.refs_3_
  76.0 1.6 shard_map.97
  77.7 1.5 collective-permute-start.3
  79.2 0.0 collective-permute-start.4
  79.2 1.7 collective-permute-start.5
  81.0 2.9 %collective-permute-start.6 = (bf16[240,128]{1,0:T(8,128)(2,1)S(1)}, bf16[240,128]{1,0:T(8,128)(2,1)S(1)}, u32[]{:S(2)}, u32[]{:S(2)}) collective-permute-start(bf16[240,128]{1,0:T(8,128)(2,1)S(1)} %get-tuple-element.42), channel_id=1, source_target_pairs={{0,16},{4,20},{8,24},{12,28},{16,0},{20,4},{24,8},{28,12},{1,17},{... | collective-permute-start | bytes 184328 | tf_op jit(solution)/shard_map/ppermute | solution.py:669
  83.8 1.2 collective-permute-start.7
  85.1 0.4 collective-permute-done.3.refs_1_
  85.4 1.4 collective-permute-start.8
  86.9 0.0 collective-permute-done.4.refs_2_
  86.9 0.8 collective-permute-start.9
  87.7 0.0 copy-done.1
  87.7 0.6 point.1.refs_10_.point_ref
  88.2 1.8 collective-permute-done.5.refs_3_
  90.0 0.4 collective-permute-done.6.refs_4_
  90.4 1.5 collective-permute-done.7.refs_5_
  91.9 0.1 collective-permute-done.8.refs_6_
  92.0 0.0 collective-permute-done.9.refs_7_
  92.0 7.5 %shard_map.98 = (bf16[240,128]{1,0:T(8,128)(2,1)S(1)}, bf16[240,128]{1,0:T(8,128)(2,1)S(1)}, bf16[240,128]{1,0:T(8,128)(2,1)S(1)}, bf16[240,128]{1,0:T(8,128)(2,...) custom-call(s32[2]{0:T(128)S(1)} %pad_add_fusion.me_ref, ...), custom_call_target="tpu_custom_call" | custom-call | tf_op jit(solution)/shard_map/pallas_call | solution.py:651
  99.6 2.1 %collective-permute-start.10 = (bf16[240,128]{1,0:T(8,128)(2,1)S(1)}, bf16[240,128]{1,0:T(8,128)(2,1)S(1)}, u32[]{:S(2)}, u32[]{:S(2)}) collective-permute-start(bf16[240,128]{1,0:T(8,128)(2,1)S(1)} %get-tuple-element.48), channel_id=1, source_target_pairs={{0,4},{4,8},{8,12},{12,16},{16,20},{20,24},{24,28},{28,0},{1,5},{5... | collective-permute-start | bytes 184328 | tf_op jit(solution)/shard_map/ppermute | solution.py:669
  101.7 2.1 %collective-permute-start.11 = (bf16[240,128]{1,0:T(8,128)(2,1)S(1)}, bf16[240,128]{1,0:T(8,128)(2,1)S(1)}, u32[]{:S(2)}, u32[]{:S(2)}) collective-permute-start(bf16[240,128]{1,0:T(8,128)(2,1)S(1)} %get-tuple-element.49), channel_id=1, source_target_pairs={{0,8},{4,12},{8,16},{12,20},{16,24},{20,28},{24,0},{28,4},{1,9},{5... | collective-permute-start | bytes 184328 | tf_op jit(solution)/shard_map/ppermute | solution.py:669
  103.8 0.6 collective-permute-start.12
  104.4 2.0 %collective-permute-start.13 = (bf16[240,128]{1,0:T(8,128)(2,1)S(1)}, bf16[240,128]{1,0:T(8,128)(2,1)S(1)}, u32[]{:S(2)}, u32[]{:S(2)}) collective-permute-start(bf16[240,128]{1,0:T(8,128)(2,1)S(1)} %get-tuple-element.51), channel_id=1, source_target_pairs={{0,16},{4,20},{8,24},{12,28},{16,0},{20,4},{24,8},{28,12},{1,17},{... | collective-permute-start | bytes 184328 | tf_op jit(solution)/shard_map/ppermute | solution.py:669
  106.4 2.5 %collective-permute-start.14 = (bf16[240,128]{1,0:T(8,128)(2,1)S(1)}, bf16[240,128]{1,0:T(8,128)(2,1)S(1)}, u32[]{:S(2)}, u32[]{:S(2)}) collective-permute-start(bf16[240,128]{1,0:T(8,128)(2,1)S(1)} %get-tuple-element.52), channel_id=1, source_target_pairs={{0,20},{4,24},{8,28},{12,0},{16,4},{20,8},{24,12},{28,16},{1,21},{... | collective-permute-start | bytes 184328 | tf_op jit(solution)/shard_map/ppermute | solution.py:669
  108.9 0.0 collective-permute-done.10.refs_1_
  108.9 1.1 collective-permute-start.15
  110.0 0.0 collective-permute-done.11.refs_2_
  110.0 1.5 collective-permute-start.16
  111.5 0.5 collective-permute-done.12.refs_3_
  112.0 1.2 collective-permute-done.13.refs_4_
  113.2 0.4 collective-permute-done.14.refs_5_
  113.6 0.9 collective-permute-done.15.refs_6_
  114.5 0.0 collective-permute-done.16.refs_7_
  114.5 1.6 shard_map.99
  116.1 0.1 collective-permute-start.17
  116.2 1.7 collective-permute-start.18
  117.8 1.4 collective-permute-start.19
  119.2 1.9 %collective-permute-done.17.refs_1_ = bf16[240,256]{1,0:T(8,128)(2,1)S(1)} collective-permute-done((bf16[240,256]{1,0:T(8,128)(2,1)S(1)}, bf16[240,256]{1,0:T(8,128)(2,1)S(1)}, u32[]{:S(2)}, u32[]{:S(2)}) %collective-permute-start.17) | collective-permute-done | bytes 122912 | tf_op jit(solution)/shard_map/ppermute | solution.py:669
  121.1 1.3 collective-permute-done.18.refs_2_
  122.4 1.1 collective-permute-done.19.refs_3_
  123.5 20.3 %shard_map.100 = (bf16[4,240,256]{2,1,0:T(8,128)(2,1)S(1)}, f32[2,4,240,128]{3,2,1,0:T(8,128)}, f32[2,20,20,24,8,32]{5,4,3,2,1,0:T(8,128)}) custom-call(s32[2]{0:T(128)S(1)} %pad_add_fusion.me_ref, bf16[240,256]{1,0:T(8,128)(2,1)S(1)} %get-tuple-element.55.refs_0_, bf16[240,256]{1,0:T(8,128)(2,1)S(1)} %collective-permute-done.17.refs_1_, ...), custom_call_target="tpu_custom_call" | custom-call | tf_op jit(solution)/shard_map/pallas_call | solution.py:651
  143.8 11.4 %all_to_all.20.refs_0_ = bf16[4,240,256]{2,1,0:T(8,128)(2,1)S(1)} all-to-all(bf16[4,240,256]{2,1,0:T(8,128)(2,1)S(1)} %get-tuple-element.60), channel_id=1, replica_groups=mesh['gx'=8,'gy'=4] {'gy'}, dimensions={0} | all-to-all | bytes 983040 | tf_op jit(solution)/shard_map/all_to_all | solution.py:732
  155.3 2.4 %shard_map.101 = bf16[8,240,128]{2,1,0:T(8,128)(2,1)} custom-call(s32[2]{0:T(128)S(1)} %pad_add_fusion.me_ref, bf16[4,240,256]{2,1,0:T(8,128)(2,1)S(1)} %all_to_all.20.refs_0_, bf16[512,512]{1,0:T(8,128)(2,1)} %constant.18.clone.refs_1_.refs_4_.refs_8_), custom_call_target="tpu_custom_call" | custom-call | tf_op jit(solution)/shard_map/pallas_call | solution.py:651
  157.6 5.7 %all-to-all-start.3 = ((bf16[8,240,128]{2,1,0:T(8,128)(2,1)}), bf16[8,240,128]{2,1,0:T(8,128)(2,1)S(1)}, u32[]{:S(2)}, u32[]{:S(2)}) async-start(bf16[8,240,128]{2,1,0:T(8,128)(2,1)} %shard_map.101), calls=%async_computation.3 | async-start | bytes 983040 | tf_op jit(solution)/shard_map/all_to_all | solution.py:729
  163.3 8.8 %shard_map.102._ = f32[2,20,20,24,8,32]{5,4,3,2,1,0:T(8,128)} custom-call(f32[2,4,240,128]{3,2,1,0:T(8,128)} %get-tuple-element.59.refs_7_.f_spec_ref, f32[2,4,240,128]{3,2,1,0:T(8,128)} %get-tuple-element.62.h_spec_ref, f32[2,20,20,24,8,32]{5,4,3,2,1,0:T(8,128)} %get-tuple-element.63._), custom_call_target="tpu_custom_call", output_to_operand_aliasing={{}: (2, {})} | custom-call | tf_op jit(solution)/shard_map/pallas_call | solution.py:780
  172.1 13.6 %shard_map.103 = f32[2,20,20,24,8,32]{5,4,3,2,1,0:T(8,128)} custom-call(f32[2,4,240,128]{3,2,1,0:T(8,128)} %get-tuple-element.59.refs_7_.f_spec_ref, f32[2,4,240,128]{3,2,1,0:T(8,128)} %get-tuple-element.62.h_spec_ref, f32[2,20,20,24,8,32]{5,4,3,2,1,0:T(8,128)} %shard_map.102._), custom_call_target="tpu_custom_call", output_to_operand_aliasing={{}: (2, {})} | custom-call | tf_op jit(solution)/shard_map/pallas_call | solution.py:780
  185.8 0.0 all-to-all-done.3.in_ref
  185.8 4.8 %final.1 = bf16[4,20,8,768]{3,2,1,0:T(8,128)(2,1)} custom-call(bf16[8,240,128]{2,1,0:T(8,128)(2,1)S(1)} %all-to-all-done.3.in_ref, bf16[640,768]{1,0:T(8,128)(2,1)} %get-tuple-element.61.hidden_ref, bf16[640,640]{1,0:T(8,128)(2,1)S(1)} %point.1.refs_10_.point_ref, bf16[2,384,768]{2,1,0:T(8,128)(2,1)} %constant.17.clone.table_ref.refs_11_), custom_call_target="tpu_custom_call" | custom-call | tf_op jit(solution)/shard_map/final/pallas_call | solution.py:812
  (2 shorter events, 0.0 us)
Async XLA Ops:
  3.7 21.1 %all-to-all-start = ((bf16[8,240,128]{2,1,0:T(8,128)(2,1)}), bf16[8,240,128]{2,1,0:T(8,128)(2,1)S(1)}, u32[]{:S(2)}, u32[]{:S(2)}) async-start(bf16[8,240,128]{2,1,0:T(8,128)(2,1)} %get-tuple-element.33), calls=%async_computation | async-start | bytes 983040 | tf_op jit(solution)/shard_map/all_to_all | solution.py:729
  27.3 29.9 %all-to-all-start.1 = ((f32[4,240,256]{2,1,0:T(8,128)}), f32[4,240,256]{2,1,0:T(8,128)S(1)}, u32[]{:S(2)}, u32[]{:S(2)}) async-start(f32[4,240,256]{2,1,0:T(8,128)} %shard_map.95), calls=%async_computation.1 | async-start | bytes 1966080 | tf_op jit(solution)/shard_map/all_to_all | solution.py:732
  46.1 11.0 %copy-start = (f32[24,128]{1,0:T(8,128)S(1)}, f32[24,128]{1,0:T(8,128)}, u32[]{:S(2)}) copy-start(f32[24,128]{1,0:T(8,128)} %constant.20.clone.refs_3_.refs_6_) | copy-start | bytes 36868
  46.1 41.5 %copy-start.1 = (bf16[20,20]{1,0:T(8,128)(2,1)S(1)}, bf16[20,20]{1,0:T(8,128)(2,1)}, u32[]{:S(2)}) copy-start(bf16[20,20]{1,0:T(8,128)(2,1)} %weight_ref.1) | copy-start | bytes 2404
  68.3 4.6 %collective-permute-start = (bf16[240,256]{1,0:T(8,128)(2,1)S(1)}, bf16[240,256]{1,0:T(8,128)(2,1)S(1)}, u32[]{:S(2)}, u32[]{:S(2)}) collective-permute-start(bf16[240,256]{1,0:T(8,128)(2,1)S(1)} %get-tuple-element.35), channel_id=1, source_target_pairs={{0,1},{1,2},{2,3},{3,0},{4,5},{5,6},{6,7},{7,4},{8,9},{9,10},{10,1... | collective-permute-start | bytes 368648 | tf_op jit(solution)/shard_map/ppermute | solution.py:669
  68.7 6.1 %collective-permute-start.1 = (bf16[240,256]{1,0:T(8,128)(2,1)S(1)}, bf16[240,256]{1,0:T(8,128)(2,1)S(1)}, u32[]{:S(2)}, u32[]{:S(2)}) collective-permute-start(bf16[240,256]{1,0:T(8,128)(2,1)S(1)} %get-tuple-element.36), channel_id=1, source_target_pairs={{0,2},{1,3},{2,0},{3,1},{4,6},{5,7},{6,4},{7,5},{8,10},{9,11},{10,... | collective-permute-start | bytes 368648 | tf_op jit(solution)/shard_map/ppermute | solution.py:669
  70.4 5.7 %collective-permute-start.2 = (bf16[240,256]{1,0:T(8,128)(2,1)S(1)}, bf16[240,256]{1,0:T(8,128)(2,1)S(1)}, u32[]{:S(2)}, u32[]{:S(2)}) collective-permute-start(bf16[240,256]{1,0:T(8,128)(2,1)S(1)} %get-tuple-element.37), channel_id=1, source_target_pairs={{0,3},{1,0},{2,1},{3,2},{4,7},{5,4},{6,5},{7,6},{8,11},{9,8},{10,9... | collective-permute-start | bytes 368648 | tf_op jit(solution)/shard_map/ppermute | solution.py:669
  77.7 7.7 %collective-permute-start.3 = (bf16[240,128]{1,0:T(8,128)(2,1)S(1)}, bf16[240,128]{1,0:T(8,128)(2,1)S(1)}, u32[]{:S(2)}, u32[]{:S(2)}) collective-permute-start(bf16[240,128]{1,0:T(8,128)(2,1)S(1)} %get-tuple-element.39), channel_id=1, source_target_pairs={{0,4},{4,8},{8,12},{12,16},{16,20},{20,24},{24,28},{28,0},{1,5},{5... | collective-permute-start | bytes 184328 | tf_op jit(solution)/shard_map/ppermute | solution.py:669
  79.2 7.7 %collective-permute-start.4 = (bf16[240,128]{1,0:T(8,128)(2,1)S(1)}, bf16[240,128]{1,0:T(8,128)(2,1)S(1)}, u32[]{:S(2)}, u32[]{:S(2)}) collective-permute-start(bf16[240,128]{1,0:T(8,128)(2,1)S(1)} %get-tuple-element.40), channel_id=1, source_target_pairs={{0,8},{4,12},{8,16},{12,20},{16,24},{20,28},{24,0},{28,4},{1,9},{5... | collective-permute-start | bytes 184328 | tf_op jit(solution)/shard_map/ppermute | solution.py:669
  79.2 10.8 %collective-permute-start.5 = (bf16[240,128]{1,0:T(8,128)(2,1)S(1)}, bf16[240,128]{1,0:T(8,128)(2,1)S(1)}, u32[]{:S(2)}, u32[]{:S(2)}) collective-permute-start(bf16[240,128]{1,0:T(8,128)(2,1)S(1)} %get-tuple-element.41), channel_id=1, source_target_pairs={{0,12},{4,16},{8,20},{12,24},{16,28},{20,0},{24,4},{28,8},{1,13},{... | collective-permute-start | bytes 184328 | tf_op jit(solution)/shard_map/ppermute | solution.py:669
  81.0 9.5 %collective-permute-start.6 = (bf16[240,128]{1,0:T(8,128)(2,1)S(1)}, bf16[240,128]{1,0:T(8,128)(2,1)S(1)}, u32[]{:S(2)}, u32[]{:S(2)}) collective-permute-start(bf16[240,128]{1,0:T(8,128)(2,1)S(1)} %get-tuple-element.42), channel_id=1, source_target_pairs={{0,16},{4,20},{8,24},{12,28},{16,0},{20,4},{24,8},{28,12},{1,17},{... | collective-permute-start | bytes 184328 | tf_op jit(solution)/shard_map/ppermute | solution.py:669
  83.8 8.1 %collective-permute-start.7 = (bf16[240,128]{1,0:T(8,128)(2,1)S(1)}, bf16[240,128]{1,0:T(8,128)(2,1)S(1)}, u32[]{:S(2)}, u32[]{:S(2)}) collective-permute-start(bf16[240,128]{1,0:T(8,128)(2,1)S(1)} %get-tuple-element.43), channel_id=1, source_target_pairs={{0,20},{4,24},{8,28},{12,0},{16,4},{20,8},{24,12},{28,16},{1,21},{... | collective-permute-start | bytes 184328 | tf_op jit(solution)/shard_map/ppermute | solution.py:669
  85.4 6.6 %collective-permute-start.8 = (bf16[240,128]{1,0:T(8,128)(2,1)S(1)}, bf16[240,128]{1,0:T(8,128)(2,1)S(1)}, u32[]{:S(2)}, u32[]{:S(2)}) collective-permute-start(bf16[240,128]{1,0:T(8,128)(2,1)S(1)} %get-tuple-element.44), channel_id=1, source_target_pairs={{0,24},{4,28},{8,0},{12,4},{16,8},{20,12},{24,16},{28,20},{1,25},{... | collective-permute-start | bytes 184328 | tf_op jit(solution)/shard_map/ppermute | solution.py:669
  86.9 5.2 %collective-permute-start.9 = (bf16[240,128]{1,0:T(8,128)(2,1)S(1)}, bf16[240,128]{1,0:T(8,128)(2,1)S(1)}, u32[]{:S(2)}, u32[]{:S(2)}) collective-permute-start(bf16[240,128]{1,0:T(8,128)(2,1)S(1)} %get-tuple-element.45), channel_id=1, source_target_pairs={{0,28},{4,0},{8,4},{12,8},{16,12},{20,16},{24,20},{28,24},{1,29},{... | collective-permute-start | bytes 184328 | tf_op jit(solution)/shard_map/ppermute | solution.py:669
  99.6 9.4 %collective-permute-start.10 = (bf16[240,128]{1,0:T(8,128)(2,1)S(1)}, bf16[240,128]{1,0:T(8,128)(2,1)S(1)}, u32[]{:S(2)}, u32[]{:S(2)}) collective-permute-start(bf16[240,128]{1,0:T(8,128)(2,1)S(1)} %get-tuple-element.48), channel_id=1, source_target_pairs={{0,4},{4,8},{8,12},{12,16},{16,20},{20,24},{24,28},{28,0},{1,5},{5... | collective-permute-start | bytes 184328 | tf_op jit(solution)/shard_map/ppermute | solution.py:669
  101.7 8.3 %collective-permute-start.11 = (bf16[240,128]{1,0:T(8,128)(2,1)S(1)}, bf16[240,128]{1,0:T(8,128)(2,1)S(1)}, u32[]{:S(2)}, u32[]{:S(2)}) collective-permute-start(bf16[240,128]{1,0:T(8,128)(2,1)S(1)} %get-tuple-element.49), channel_id=1, source_target_pairs={{0,8},{4,12},{8,16},{12,20},{16,24},{20,28},{24,0},{28,4},{1,9},{5... | collective-permute-start | bytes 184328 | tf_op jit(solution)/shard_map/ppermute | solution.py:669
  103.8 8.2 %collective-permute-start.12 = (bf16[240,128]{1,0:T(8,128)(2,1)S(1)}, bf16[240,128]{1,0:T(8,128)(2,1)S(1)}, u32[]{:S(2)}, u32[]{:S(2)}) collective-permute-start(bf16[240,128]{1,0:T(8,128)(2,1)S(1)} %get-tuple-element.50), channel_id=1, source_target_pairs={{0,12},{4,16},{8,20},{12,24},{16,28},{20,0},{24,4},{28,8},{1,13},{... | collective-permute-start | bytes 184328 | tf_op jit(solution)/shard_map/ppermute | solution.py:669
  104.4 8.7 %collective-permute-start.13 = (bf16[240,128]{1,0:T(8,128)(2,1)S(1)}, bf16[240,128]{1,0:T(8,128)(2,1)S(1)}, u32[]{:S(2)}, u32[]{:S(2)}) collective-permute-start(bf16[240,128]{1,0:T(8,128)(2,1)S(1)} %get-tuple-element.51), channel_id=1, source_target_pairs={{0,16},{4,20},{8,24},{12,28},{16,0},{20,4},{24,8},{28,12},{1,17},{... | collective-permute-start | bytes 184328 | tf_op jit(solution)/shard_map/ppermute | solution.py:669
  106.4 7.2 %collective-permute-start.14 = (bf16[240,128]{1,0:T(8,128)(2,1)S(1)}, bf16[240,128]{1,0:T(8,128)(2,1)S(1)}, u32[]{:S(2)}, u32[]{:S(2)}) collective-permute-start(bf16[240,128]{1,0:T(8,128)(2,1)S(1)} %get-tuple-element.52), channel_id=1, source_target_pairs={{0,20},{4,24},{8,28},{12,0},{16,4},{20,8},{24,12},{28,16},{1,21},{... | collective-permute-start | bytes 184328 | tf_op jit(solution)/shard_map/ppermute | solution.py:669
  108.9 5.5 %collective-permute-start.15 = (bf16[240,128]{1,0:T(8,128)(2,1)S(1)}, bf16[240,128]{1,0:T(8,128)(2,1)S(1)}, u32[]{:S(2)}, u32[]{:S(2)}) collective-permute-start(bf16[240,128]{1,0:T(8,128)(2,1)S(1)} %get-tuple-element.53), channel_id=1, source_target_pairs={{0,24},{4,28},{8,0},{12,4},{16,8},{20,12},{24,16},{28,20},{1,25},{... | collective-permute-start | bytes 184328 | tf_op jit(solution)/shard_map/ppermute | solution.py:669
  110.0 4.5 %collective-permute-start.16 = (bf16[240,128]{1,0:T(8,128)(2,1)S(1)}, bf16[240,128]{1,0:T(8,128)(2,1)S(1)}, u32[]{:S(2)}, u32[]{:S(2)}) collective-permute-start(bf16[240,128]{1,0:T(8,128)(2,1)S(1)} %get-tuple-element.54), channel_id=1, source_target_pairs={{0,28},{4,0},{8,4},{12,8},{16,12},{20,16},{24,20},{28,24},{1,29},{... | collective-permute-start | bytes 184328 | tf_op jit(solution)/shard_map/ppermute | solution.py:669
  116.1 5.0 %collective-permute-start.17 = (bf16[240,256]{1,0:T(8,128)(2,1)S(1)}, bf16[240,256]{1,0:T(8,128)(2,1)S(1)}, u32[]{:S(2)}, u32[]{:S(2)}) collective-permute-start(bf16[240,256]{1,0:T(8,128)(2,1)S(1)} %get-tuple-element.56), channel_id=1, source_target_pairs={{0,1},{1,2},{2,3},{3,0},{4,5},{5,6},{6,7},{7,4},{8,9},{9,10},{10,1... | collective-permute-start | bytes 368648 | tf_op jit(solution)/shard_map/ppermute | solution.py:669
  116.2 6.3 %collective-permute-start.18 = (bf16[240,256]{1,0:T(8,128)(2,1)S(1)}, bf16[240,256]{1,0:T(8,128)(2,1)S(1)}, u32[]{:S(2)}, u32[]{:S(2)}) collective-permute-start(bf16[240,256]{1,0:T(8,128)(2,1)S(1)} %get-tuple-element.57), channel_id=1, source_target_pairs={{0,2},{1,3},{2,0},{3,1},{4,6},{5,7},{6,4},{7,5},{8,10},{9,11},{10,... | collective-permute-start | bytes 368648 | tf_op jit(solution)/shard_map/ppermute | solution.py:669
  117.8 5.7 %collective-permute-start.19 = (bf16[240,256]{1,0:T(8,128)(2,1)S(1)}, bf16[240,256]{1,0:T(8,128)(2,1)S(1)}, u32[]{:S(2)}, u32[]{:S(2)}) collective-permute-start(bf16[240,256]{1,0:T(8,128)(2,1)S(1)} %get-tuple-element.58), channel_id=1, source_target_pairs={{0,3},{1,0},{2,1},{3,2},{4,7},{5,4},{6,5},{7,6},{8,11},{9,8},{10,9... | collective-permute-start | bytes 368648 | tf_op jit(solution)/shard_map/ppermute | solution.py:669
  157.6 28.1 %all-to-all-start.3 = ((bf16[8,240,128]{2,1,0:T(8,128)(2,1)}), bf16[8,240,128]{2,1,0:T(8,128)(2,1)S(1)}, u32[]{:S(2)}, u32[]{:S(2)}) async-start(bf16[8,240,128]{2,1,0:T(8,128)(2,1)} %shard_map.101), calls=%async_computation.3 | async-start | bytes 983040 | tf_op jit(solution)/shard_map/all_to_all | solution.py:729
